TPU v7x, 32 devices: a whole 2x2x4 slice. The times are simulated.
32 devices in a mesh: level: 2 (over y), space: 4 (over z), col: 4 (over x, core).
Axes of the slice: x: 2, y: 2, z: 4, core: 2. Of those that a mesh axis runs over, the one named last changes fastest.
Arguments:
- emission: bfloat16 [512, 4096], P(('level', 'space', 'col')), parts along dimension 0, may hold values from 0.049804688 to 5
- reflect: float32 [32768], P(('level', 'space', 'col')), parts along dimension 0, may hold values from 0.2 to 0.9
- form_blocks: bfloat16 [512, 4, 4, 4096], P(('level', 'space'), 'col'), parts along dimension 0, may hold values from 0 to 0.03125
- block_rows: int32 [512, 4, 4], P(('level', 'space'), 'col'), parts along dimension 0, may hold values from 0 to 255, as said below
- view_grads: bfloat16 [8, 4, 4, 4, 4096], P(('level', 'space'), 'col'), parts along dimension 0, may hold values from -0.5 to 1.5
- view_rows: int32 [8, 4, 4, 4], P(('level', 'space'), 'col'), parts along dimension 0, may hold values from 0 to 63
- view_counts: int32 [8, 4, 4], P(('level', 'space'), 'col'), parts along dimension 0, may hold values from 1 to 4, as said below
Outputs:
- grad_emission: float32 [512, 4096], P(('level', 'space', 'col')), parts along dimension 0
- grad_reflect: float32 [32768], P(('level', 'space', 'col')), parts along dimension 0
There are 2 independent parts, one for each index of `level`. A program takes and returns all parts, laid end to end along the dimension named above; each array names one. Nothing has to cross between parts.
Inputs may be any that keep to these rules, and one draw needn't show every extreme that they name: `block_rows`: the receiving block row of column block j lies in the same or an adjacent run of 64 blocks as j. `view_counts`: in every draw one owner receives 4 entries from every sender.
All inputs are finite; a program needn't handle non-finite values.
Results may differ from a plain program's by a relative error of at most 0.0003.
Values may be sent and summed in bfloat16 or wider, within the bound.
A program may use at most 128 MiB of HBM per device.

v0:
```python
import jax
import jax.numpy as jnp
from jax import lax
from jax.sharding import PartitionSpec as P

BLK = 64
CONF = 64


def passed_along(block, axis, distance):
    devices = range(lax.axis_size(axis))
    route = [(i - distance, i) for i in devices if i - distance in devices]
    return lax.ppermute(block, axis, route)


def extended(shard, sides, width):
    for axis, dim in sides:
        count, length = (lax.axis_size(axis), shard.shape[dim])
        up = [(i, (i + 1) % count) for i in range(count - 1)]
        down = [(j, i) for i, j in up]
        last = lax.slice_in_dim(shard, length - width, length, axis=dim)
        first = lax.slice_in_dim(shard, 0, width, axis=dim)
        before = lax.ppermute(last, axis, up)
        after = lax.ppermute(first, axis, down)
        shard = jnp.concatenate([before, shard, after], axis=dim)
    return shard


def col_sums(array):
    return lax.psum_scatter(array, "col", scatter_dimension=1, tiled=True)


def col_rows(array):
    return lax.all_gather(array, "col", axis=1, tiled=True)


def pass_rows(array, offset):
    return passed_along(array.astype(jnp.bfloat16), "space", offset).astype(array.dtype)


def spread_rows(array):
    return extended(array, (("space", 1),), array.shape[1])


def forward(blocks, window_index, sources):
    rows_dev = blocks.shape[0]
    block_terms = jnp.einsum(
        "jkab,jbl->jkal",
        blocks,
        sources.reshape(rows_dev, BLK, CONF),
        preferred_element_type=jnp.float32,
    )
    window = (
        jnp.zeros((3 * rows_dev, BLK * CONF), jnp.float32)
        .at[window_index]
        .add(block_terms.reshape(-1, BLK * CONF))
    )
    window = window.reshape(3, rows_dev, BLK * CONF)
    own_sums = window[1] + pass_rows(window[0], -1) + pass_rows(window[2], 1)
    return col_sums(own_sums[None])[0]


def adjoint(blocks, window_index, scaled):
    rows_dev = blocks.shape[0]
    slots_dev = blocks.shape[1]
    window = spread_rows(col_rows(scaled[None]))
    window = window.reshape(3 * rows_dev, BLK * CONF)
    picked = window[window_index].reshape(rows_dev, slots_dev, BLK, CONF)
    adjoint_terms = jnp.einsum("jkab,jkal->jbl", blocks, picked, preferred_element_type=jnp.float32)
    return col_sums(adjoint_terms.reshape(1, rows_dev, BLK * CONF))[0]


def body(emission, reflect, form_blocks, block_rows, view_grads, view_rows, view_counts):
    rows_dev = form_blocks.shape[0]
    slots_dev = form_blocks.shape[2]
    piece_rows = emission.shape[0]
    shard_index = lax.axis_index("space")
    blocks = form_blocks.reshape(rows_dev, slots_dev, BLK, BLK)
    window_index = block_rows.reshape(rows_dev * slots_dev) - (shard_index - 1) * rows_dev
    gain_rows = reflect.reshape(piece_rows, BLK, 1)
    arrived = (
        lax.all_to_all(view_grads, "space", split_axis=2, concat_axis=2, tiled=True),
        lax.all_to_all(view_rows, "space", split_axis=2, concat_axis=2, tiled=True),
        lax.all_to_all(view_counts, "space", split_axis=2, concat_axis=2, tiled=True),
    )
    arrived_grads, arrived_rows, arrived_counts = arrived
    slot_index = lax.broadcasted_iota(jnp.int32, arrived_rows.shape, 3)
    live_slots = slot_index < arrived_counts[..., None]
    slot_values = jnp.where(live_slots[..., None], arrived_grads.astype(jnp.float32), 0.0).reshape(
        -1, BLK * CONF
    )
    view_local = (
        jnp.zeros((rows_dev, BLK * CONF), jnp.float32).at[arrived_rows.reshape(-1)].add(slot_values)
    )
    view_total = col_sums(view_local[None])[0]
    first_sums = forward(blocks, window_index, col_rows(emission[None])[0])
    emitted = emission.astype(jnp.float32).reshape(piece_rows, BLK, CONF)
    bounced = (
        (emitted + gain_rows * first_sums.reshape(piece_rows, BLK, CONF))
        .reshape(piece_rows, BLK * CONF)
        .astype(jnp.bfloat16)
    )
    second_sums = forward(blocks, window_index, col_rows(bounced[None])[0])
    scaled_one = (
        (gain_rows * view_total.reshape(piece_rows, BLK, CONF))
        .reshape(piece_rows, BLK * CONF)
        .astype(jnp.bfloat16)
    )
    adjoint_one = adjoint(blocks, window_index, scaled_one)
    scaled_two = (
        (gain_rows * adjoint_one.reshape(piece_rows, BLK, CONF))
        .reshape(piece_rows, BLK * CONF)
        .astype(jnp.bfloat16)
    )
    adjoint_two = adjoint(blocks, window_index, scaled_two)
    grad_emission = view_total + adjoint_one + adjoint_two
    product = view_total * second_sums + adjoint_one * first_sums
    grad_reflect = product.reshape(piece_rows, BLK, CONF).sum(axis=2).reshape(piece_rows * BLK)
    return (grad_emission, grad_reflect)


def solution(mesh):
    in_specs = (
        P(("level", "space", "col"), None),
        P(("level", "space", "col")),
        P(("level", "space"), "col", None, None),
        P(("level", "space"), "col", None),
        P(("level", "space"), "col", None, None, None),
        P(("level", "space"), "col", None, None),
        P(("level", "space"), "col", None),
    )
    out_specs = (P(("level", "space", "col"), None), P(("level", "space", "col")))
    return jax.shard_map(body, mesh=mesh, in_specs=in_specs, out_specs=out_specs, check_vma=False)
```

profile of v0, /device:TPU:0, one launch (start us, length us, event | category | flops | bytes accessed | tf_op | source)
XLA Modules:
  0.0 302.7 jit_solution(5888415756539695728)
XLA Ops:
  8.6 6.3 %all-to-all-start.1 = ((s32[1,1,4]{1,0,2:T(1,128)}), s32[1,1,4]{1,0,2:T(1,128)S(1)}, u32[]{:S(2)}, u32[]{:S(2)}) async-start(s32[1,1,4]{1,0,2:T(1,128)} %copy.29), calls=%async_computation.1 | async-start | bytes 4096 | tf_op jit(solution)/shard_map/all_to_all | solution.py:84
  15.9 8.5 %all-gather = bf16[64,4096]{1,0:T(8,128)(2,1)} all-gather(bf16[16,4096]{1,0:T(8,128)(2,1)} %param.7), channel_id=2, replica_groups=mesh['level'=2,'space'=4,'col'=4] {'col'}, dimensions={0}, use_global_device_ids=true | all-gather | bytes 655360 | tf_op jit(solution)/shard_map/all_gather | solution.py:34
  26.4 4.5 %reshape.158 = bf16[64,4,64,64]{3,2,1,0:T(8,128)(2,1)} reshape(bf16[64,1,4,4096]{3,2,1,0:T(4,128)(2,1)S(1)} %copy-done.2) | data formatting | bytes 4194304 | tf_op jit(solution)/shard_map/reshape | solution.py:78
  30.9 6.7 %fusion.9 = f32[64,4,64,64]{3,2,1,0:T(8,128)} fusion(bf16[64,4,64,64]{3,2,1,0:T(8,128)(2,1)} %reshape.158, bf16[64,64,64,1]{2,1,0,3:T(8,128)(2,1)S(1)} %reshape.212), kind=kOutput, calls=%fused_computation.21 | convolution fusion | flops 134217728 | bytes 6815744 | tf_op jit(solution)/shard_map/jkab,jbl->jkal/dot_general | solution.py:47
  37.5 7.9 %reshape.194 = f32[256,4096]{1,0:T(8,128)} reshape(f32[64,4,64,64]{3,2,1,0:T(8,128)} %fusion.9) | data formatting | bytes 8388608 | tf_op jit(solution)/shard_map/reshape | solution.py:56
  45.5 8.3 %scatter_custom_fusion.1 = f32[192,4096]{1,0:T(8,128)S(1)} fusion(s32[256]{0:T(256)S(1)} %bitcast.58, f32[256,4096]{1,0:T(8,128)} %reshape.194, f32[]{:T(128)} %constant.7.clone.1), kind=kCustom, calls=%fused_computation.12 | custom fusion | flops 1048576 | bytes 3146240 | tf_op jit(solution)/shard_map/scatter-add | solution.py:56
  55.1 4.8 %all-to-all-start = ((s32[1,1,4,4]{3,1,0,2:T(1,128)}), s32[1,1,4,4]{3,1,0,2:T(1,128)S(1)}, u32[]{:S(2)}, u32[]{:S(2)}) async-start(s32[1,1,4,4]{3,1,0,2:T(1,128)} %bitcast), calls=%async_computation | async-start | bytes 4096 | tf_op jit(solution)/shard_map/all_to_all | solution.py:83
  60.1 5.2 %all-to-all-done = s32[1,1,4,4]{3,1,0,2:T(1,128)S(1)} async-done(((s32[1,1,4,4]{3,1,0,2:T(1,128)}), s32[1,1,4,4]{3,1,0,2:T(1,128)S(1)}, u32[]{:S(2)}, u32[]{:S(2)}) %all-to-all-start) | async-done | bytes 96 | tf_op jit(solution)/shard_map/all_to_all | solution.py:83
  65.4 3.3 %all-to-all-start.2 = ((bf16[1,1,4,4,4096]{4,3,1,0,2:T(4,128)(2,1)}), bf16[1,1,4,4,4096]{4,3,1,0,2:T(4,128)(2,1)S(1)}, u32[]{:S(2)}, u32[]{:S(2)}) async-start(bf16[1,1,4,4,4096]{4,3,1,0,2:T(4,128)(2,1)} %bitcast.2), calls=%async_computation.2 | async-start | bytes 262144 | tf_op jit(solution)/shard_map/all_to_all | solution.py:82
  70.0 4.6 %all-to-all-done.2 = bf16[1,1,4,4,4096]{4,3,1,0,2:T(4,128)(2,1)S(1)} async-done(((bf16[1,1,4,4,4096]{4,3,1,0,2:T(4,128)(2,1)}), bf16[1,1,4,4,4096]{4,3,1,0,2:T(4,128)(2,1)S(1)}, u32[]{:S(2)}, u32[]{:S(2)}) %all-to-all-start.2) | async-done | bytes 131104 | tf_op jit(solution)/shard_map/all_to_all | solution.py:82
  80.5 4.9 %collective-permute-start.5 = (bf16[64,4096]{1,0:T(8,128)(2,1)S(1)}, bf16[64,4096]{1,0:T(8,128)(2,1)S(1)}, u32[]{:S(2)}, u32[]{:S(2)}) collective-permute-start(bf16[64,4096]{1,0:T(8,128)(2,1)S(1)} %get-tuple-element.5), channel_id=1, source_target_pairs={{0,4},{4,8},{8,12},{1,5},{5,9},{9,13},{2,6},{6,10},{10,14},{3,7},{... | collective-permute-start | bytes 1572872 | tf_op jit(solution)/shard_map/ppermute | solution.py:13
  85.4 7.3 %collective-permute-done.4 = bf16[64,4096]{1,0:T(8,128)(2,1)S(1)} collective-permute-done((bf16[64,4096]{1,0:T(8,128)(2,1)S(1)}, bf16[64,4096]{1,0:T(8,128)(2,1)S(1)}, u32[]{:S(2)}, u32[]{:S(2)}) %collective-permute-start.4) | collective-permute-done | bytes 524320 | tf_op jit(solution)/shard_map/ppermute | solution.py:13
  95.9 5.2 %reduce-scatter.6.cloned.1.call-done = f32[1,16,4096]{2,1,0:T(8,128)} async-done(((f32[1,64,4096]{2,1,0:T(8,128)}), f32[1,16,4096]{2,1,0:T(8,128)}) %reduce-scatter.6.cloned.1.call-update) | async-done | bytes 262160 | tf_op jit(solution)/shard_map/reduce_scatter | solution.py:30
  102.0 7.2 %all_gather.12 = bf16[1,64,4096]{2,1,0:T(8,128)(2,1)} all-gather(bf16[1,16,4096]{2,1,0:T(8,128)(2,1)S(1)} %multiply_convert_fusion.1), channel_id=1, replica_groups=mesh['level'=2,'space'=4,'col'=4] {'col'}, dimensions={1}, use_global_device_ids=true | all-gather | bytes 655360 | tf_op jit(solution)/shard_map/all_gather | solution.py:34
  110.5 5.4 %collective-permute-start = (bf16[1,64,4096]{2,1,0:T(8,128)(2,1)}, bf16[1,64,4096]{2,1,0:T(8,128)(2,1)}, u32[]{:S(2)}, u32[]{:S(2)}) collective-permute-start(bf16[1,64,4096]{2,1,0:T(8,128)(2,1)} %all_gather.12), channel_id=1, source_target_pairs={{0,4},{4,8},{8,12},{1,5},{5,9},{9,13},{2,6},{6,10},{10,14},{3,7},{... | collective-permute-start | bytes 1572872 | tf_op jit(solution)/shard_map/ppermute | solution.py:23
  115.9 12.8 %reduce-scatter.12.cloned.1.call-done = f32[1,16,4096]{2,1,0:T(8,128)} async-done(((f32[1,64,4096]{2,1,0:T(8,128)}), f32[1,16,4096]{2,1,0:T(8,128)}) %reduce-scatter.12.cloned.1.call-update) | async-done | bytes 262160 | tf_op jit(solution)/shard_map/reduce_scatter | solution.py:30
  129.7 6.8 %all-gather.1 = bf16[64,4096]{1,0:T(8,128)(2,1)S(1)} all-gather(bf16[16,4096]{1,0:T(8,128)(2,1)S(1)} %fusion.14), channel_id=3, replica_groups=mesh['level'=2,'space'=4,'col'=4] {'col'}, dimensions={0}, use_global_device_ids=true | all-gather | bytes 655360 | tf_op jit(solution)/shard_map/all_gather | solution.py:34
  137.6 9.5 %convolution_bitcast_fusion = f32[64,4,64,64]{2,3,1,0:T(8,128)} fusion(bf16[64,4,64,64]{3,2,1,0:T(8,128)(2,1)} %reshape.158, bf16[64,64,64]{2,1,0:T(8,128)(2,1)S(1)} %reshape_squeeze.13), kind=kOutput, calls=%fused_computation.5 | convolution fusion | flops 134217728 | bytes 6815744 | tf_op jit(solution)/shard_map/jkab,jbl->jkal/dot_general | solution.py:47
  147.1 9.0 %copy.37 = f32[64,4,64,64]{3,2,1,0:T(8,128)} copy(f32[64,4,64,64]{2,3,1,0:T(8,128)} %convolution_bitcast_fusion) | data formatting | bytes 8388608 | tf_op jit(solution)/shard_map/jkab,jbl->jkal/dot_general | solution.py:47
  156.1 7.9 %reshape.202 = f32[256,4096]{1,0:T(8,128)} reshape(f32[64,4,64,64]{3,2,1,0:T(8,128)} %copy.37) | data formatting | bytes 8388608 | tf_op jit(solution)/shard_map/reshape | solution.py:56
  164.1 8.5 %scatter_custom_fusion.2 = f32[192,4096]{1,0:T(8,128)S(1)} fusion(s32[256]{0:T(256)S(1)} %bitcast.60, f32[256,4096]{1,0:T(8,128)} %reshape.202, f32[]{:T(128)} %constant.7.clone.1), kind=kCustom, calls=%fused_computation.10 | custom fusion | flops 1048576 | bytes 3146240 | tf_op jit(solution)/shard_map/scatter-add | solution.py:56
  179.5 6.9 %reshape.157 = bf16[64,4,64,64]{3,2,1,0:T(8,128)(2,1)} reshape(bf16[256,4096]{1,0:T(8,128)(2,1)} %gather_fusion) | data formatting | bytes 4194304 | tf_op jit(solution)/shard_map/reshape | solution.py:68
  186.4 5.0 %convolution_bitcast_fusion.2 = f32[64,64,64]{1,2,0:T(8,128)S(1)} fusion(bf16[64,4,64,64]{3,2,1,0:T(8,128)(2,1)} %reshape.157, bf16[64,4,64,64]{3,2,1,0:T(8,128)(2,1)} %reshape.158), kind=kOutput, calls=%fused_computation.7 | convolution fusion | flops 134217728 | bytes 5242880 | tf_op jit(solution)/shard_map/jkab,jkal->jbl/dot_general | solution.py:69
  197.8 4.6 %collective-permute-start.7 = (bf16[64,4096]{1,0:T(8,128)(2,1)S(1)}, bf16[64,4096]{1,0:T(8,128)(2,1)S(1)}, u32[]{:S(2)}, u32[]{:S(2)}) collective-permute-start(bf16[64,4096]{1,0:T(8,128)(2,1)S(1)} %get-tuple-element.3), channel_id=1, source_target_pairs={{0,4},{4,8},{8,12},{1,5},{5,9},{9,13},{2,6},{6,10},{10,14},{3,7},{... | collective-permute-start | bytes 1572872 | tf_op jit(solution)/shard_map/ppermute | solution.py:13
  202.4 10.2 %collective-permute-done.6 = bf16[64,4096]{1,0:T(8,128)(2,1)S(1)} collective-permute-done((bf16[64,4096]{1,0:T(8,128)(2,1)S(1)}, bf16[64,4096]{1,0:T(8,128)(2,1)S(1)}, u32[]{:S(2)}, u32[]{:S(2)}) %collective-permute-start.6) | collective-permute-done | bytes 524320 | tf_op jit(solution)/shard_map/ppermute | solution.py:13
  216.2 5.6 %reduce-scatter.8.cloned.1.call-done = f32[1,16,4096]{2,1,0:T(8,128)} async-done(((f32[1,64,4096]{2,1,0:T(8,128)}), f32[1,16,4096]{2,1,0:T(8,128)}) %reduce-scatter.8.cloned.1.call-update) | async-done | bytes 262160 | tf_op jit(solution)/shard_map/reduce_scatter | solution.py:30
  222.8 6.8 %all_gather.13 = bf16[1,64,4096]{2,1,0:T(8,128)(2,1)S(1)} all-gather(bf16[1,16,4096]{2,1,0:T(8,128)(2,1)S(1)} %multiply_convert_fusion), channel_id=1, replica_groups=mesh['level'=2,'space'=4,'col'=4] {'col'}, dimensions={1}, use_global_device_ids=true | all-gather | bytes 655360 | tf_op jit(solution)/shard_map/all_gather | solution.py:34
  230.8 4.6 %collective-permute-start.2 = (bf16[1,64,4096]{2,1,0:T(8,128)(2,1)S(1)}, bf16[1,64,4096]{2,1,0:T(8,128)(2,1)S(1)}, u32[]{:S(2)}, u32[]{:S(2)}) collective-permute-start(bf16[1,64,4096]{2,1,0:T(8,128)(2,1)S(1)} %all_gather.13), channel_id=1, source_target_pairs={{0,4},{4,8},{8,12},{1,5},{5,9},{9,13},{2,6},{6,10},{10,14},{3,7},{... | collective-permute-start | bytes 1572872 | tf_op jit(solution)/shard_map/ppermute | solution.py:23
  235.4 10.2 %collective-permute-done.3 = bf16[1,64,4096]{2,1,0:T(8,128)(2,1)S(1)} collective-permute-done((bf16[1,64,4096]{2,1,0:T(8,128)(2,1)S(1)}, bf16[1,64,4096]{2,1,0:T(8,128)(2,1)S(1)}, u32[]{:S(2)}, u32[]{:S(2)}) %collective-permute-start.3) | collective-permute-done | bytes 524320 | tf_op jit(solution)/shard_map/ppermute | solution.py:24
  250.1 6.9 %reshape.161 = bf16[64,4,64,64]{3,2,1,0:T(8,128)(2,1)} reshape(bf16[256,4096]{1,0:T(8,128)(2,1)} %gather_fusion.1) | data formatting | bytes 4194304 | tf_op jit(solution)/shard_map/reshape | solution.py:68
  256.9 5.0 %convolution_bitcast_fusion.1 = f32[64,64,64]{1,2,0:T(8,128)S(1)} fusion(bf16[64,4,64,64]{3,2,1,0:T(8,128)(2,1)} %reshape.161, bf16[64,4,64,64]{3,2,1,0:T(8,128)(2,1)} %reshape.158), kind=kOutput, calls=%fused_computation.6 | convolution fusion | flops 134217728 | bytes 5242880 | tf_op jit(solution)/shard_map/jkab,jkal->jbl/dot_general | solution.py:69
  266.8 26.4 %reduce-scatter.10.cloned.1.call-done = f32[1,16,4096]{2,1,0:T(8,128)} async-done(((f32[1,64,4096]{2,1,0:T(8,128)}), f32[1,16,4096]{2,1,0:T(8,128)}) %reduce-scatter.10.cloned.1.call-update) | async-done | bytes 262160 | tf_op jit(solution)/shard_map/reduce_scatter | solution.py:30
  (79 shorter events, 52.1 us)
Async XLA Ops:
  7.2 19.2 %copy-start.2 = (bf16[64,1,4,4096]{3,2,1,0:T(4,128)(2,1)S(1)}, bf16[64,1,4,4096]{3,2,1,0:T(4,128)(2,1)}, u32[]{:S(2)}) copy-start(bf16[64,1,4,4096]{3,2,1,0:T(4,128)(2,1)} %param.9) | copy-start | bytes 6291460
  8.6 46.5 %all-to-all-start.1 = ((s32[1,1,4]{1,0,2:T(1,128)}), s32[1,1,4]{1,0,2:T(1,128)S(1)}, u32[]{:S(2)}, u32[]{:S(2)}) async-start(s32[1,1,4]{1,0,2:T(1,128)} %copy.29), calls=%async_computation.1 | async-start | bytes 4096 | tf_op jit(solution)/shard_map/all_to_all | solution.py:84
  55.1 10.3 %all-to-all-start = ((s32[1,1,4,4]{3,1,0,2:T(1,128)}), s32[1,1,4,4]{3,1,0,2:T(1,128)S(1)}, u32[]{:S(2)}, u32[]{:S(2)}) async-start(s32[1,1,4,4]{3,1,0,2:T(1,128)} %bitcast), calls=%async_computation | async-start | bytes 4096 | tf_op jit(solution)/shard_map/all_to_all | solution.py:83
  65.4 9.2 %all-to-all-start.2 = ((bf16[1,1,4,4,4096]{4,3,1,0,2:T(4,128)(2,1)}), bf16[1,1,4,4,4096]{4,3,1,0,2:T(4,128)(2,1)S(1)}, u32[]{:S(2)}, u32[]{:S(2)}) async-start(bf16[1,1,4,4,4096]{4,3,1,0,2:T(4,128)(2,1)} %bitcast.2), calls=%async_computation.2 | async-start | bytes 262144 | tf_op jit(solution)/shard_map/all_to_all | solution.py:82
  68.7 32.3 %reduce-scatter.6.cloned.1.call-start = ((), (), s32[]{:S(2)}) async-start(), calls=%async_computation.8 | async-start | bytes 1310720 | tf_op jit(solution)/shard_map/reduce_scatter | solution.py:30
  77.9 17.3 %copy-start.7 = (f32[1024]{0:T(1024)S(1)}, f32[1024]{0:T(1024)}, u32[]{:S(2)}) copy-start(f32[1024]{0:T(1024)} %param.8) | copy-start | bytes 12292
  77.9 50.8 %reduce-scatter.12.cloned.1.call-start = ((), (), s32[]{:S(2)}) async-start(), calls=%async_computation.11 | async-start | bytes 1310720 | tf_op jit(solution)/shard_map/reduce_scatter | solution.py:30
  79.2 13.5 %collective-permute-start.4 = (bf16[64,4096]{1,0:T(8,128)(2,1)S(1)}, bf16[64,4096]{1,0:T(8,128)(2,1)S(1)}, u32[]{:S(2)}, u32[]{:S(2)}) collective-permute-start(bf16[64,4096]{1,0:T(8,128)(2,1)S(1)} %get-tuple-element.4), channel_id=1, source_target_pairs={{4,0},{8,4},{12,8},{5,1},{9,5},{13,9},{6,2},{10,6},{14,10},{7,3},{... | collective-permute-start | bytes 1572872 | tf_op jit(solution)/shard_map/ppermute | solution.py:13
  80.5 48.2 %copy-start.6 = (bf16[16,4096]{1,0:T(8,128)(2,1)S(1)}, bf16[16,4096]{1,0:T(8,128)(2,1)}, u32[]{:S(2)}) copy-start(bf16[16,4096]{1,0:T(8,128)(2,1)} %param.7) | copy-start | bytes 393220
  80.5 13.5 %collective-permute-start.5 = (bf16[64,4096]{1,0:T(8,128)(2,1)S(1)}, bf16[64,4096]{1,0:T(8,128)(2,1)S(1)}, u32[]{:S(2)}, u32[]{:S(2)}) collective-permute-start(bf16[64,4096]{1,0:T(8,128)(2,1)S(1)} %get-tuple-element.5), channel_id=1, source_target_pairs={{0,4},{4,8},{8,12},{1,5},{5,9},{9,13},{2,6},{6,10},{10,14},{3,7},{... | collective-permute-start | bytes 1572872 | tf_op jit(solution)/shard_map/ppermute | solution.py:13
  95.2 126.6 %reduce-scatter.8.cloned.1.call-start = ((), (), s32[]{:S(2)}) async-start(), calls=%async_computation.9 | async-start | bytes 1310720 | tf_op jit(solution)/shard_map/reduce_scatter | solution.py:30
  109.3 64.8 %collective-permute-start.1 = (bf16[1,64,4096]{2,1,0:T(8,128)(2,1)}, bf16[1,64,4096]{2,1,0:T(8,128)(2,1)}, u32[]{:S(2)}, u32[]{:S(2)}) collective-permute-start(bf16[1,64,4096]{2,1,0:T(8,128)(2,1)} %all_gather.12), channel_id=1, source_target_pairs={{4,0},{8,4},{12,8},{5,1},{9,5},{13,9},{6,2},{10,6},{14,10},{7,3},{... | collective-permute-start | bytes 1572872 | tf_op jit(solution)/shard_map/ppermute | solution.py:24
  110.5 64.3 %collective-permute-start = (bf16[1,64,4096]{2,1,0:T(8,128)(2,1)}, bf16[1,64,4096]{2,1,0:T(8,128)(2,1)}, u32[]{:S(2)}, u32[]{:S(2)}) collective-permute-start(bf16[1,64,4096]{2,1,0:T(8,128)(2,1)} %all_gather.12), channel_id=1, source_target_pairs={{0,4},{4,8},{8,12},{1,5},{5,9},{9,13},{2,6},{6,10},{10,14},{3,7},{... | collective-permute-start | bytes 1572872 | tf_op jit(solution)/shard_map/ppermute | solution.py:23
  172.5 2.3 copy-start
  193.2 3.2 %copy-start.1 = (bf16[192,4096]{1,0:T(8,128)(2,1)S(1)}, bf16[192,4096]{1,0:T(8,128)(2,1)}, u32[]{:S(2)}) copy-start(bf16[192,4096]{1,0:T(8,128)(2,1)} %convert.9) | copy-start | bytes 4718596
  196.3 70.5 %reduce-scatter.14.cloned.1.call-start = ((), (), s32[]{:S(2)}) async-start(), calls=%async_computation.12 | async-start | bytes 1310720 | tf_op jit(solution)/shard_map/reduce_scatter | solution.py:30
  196.5 16.1 %collective-permute-start.6 = (bf16[64,4096]{1,0:T(8,128)(2,1)S(1)}, bf16[64,4096]{1,0:T(8,128)(2,1)S(1)}, u32[]{:S(2)}, u32[]{:S(2)}) collective-permute-start(bf16[64,4096]{1,0:T(8,128)(2,1)S(1)} %get-tuple-element.2), channel_id=1, source_target_pairs={{4,0},{8,4},{12,8},{5,1},{9,5},{13,9},{6,2},{10,6},{14,10},{7,3},{... | collective-permute-start | bytes 1572872 | tf_op jit(solution)/shard_map/ppermute | solution.py:13
  197.8 16.0 %collective-permute-start.7 = (bf16[64,4096]{1,0:T(8,128)(2,1)S(1)}, bf16[64,4096]{1,0:T(8,128)(2,1)S(1)}, u32[]{:S(2)}, u32[]{:S(2)}) collective-permute-start(bf16[64,4096]{1,0:T(8,128)(2,1)S(1)} %get-tuple-element.3), channel_id=1, source_target_pairs={{0,4},{4,8},{8,12},{1,5},{5,9},{9,13},{2,6},{6,10},{10,14},{3,7},{... | collective-permute-start | bytes 1572872 | tf_op jit(solution)/shard_map/ppermute | solution.py:13
  216.2 77.1 %reduce-scatter.10.cloned.1.call-start = ((), (), s32[]{:S(2)}) async-start(), calls=%async_computation.10 | async-start | bytes 1310720 | tf_op jit(solution)/shard_map/reduce_scatter | solution.py:30
  229.5 16.1 %collective-permute-start.3 = (bf16[1,64,4096]{2,1,0:T(8,128)(2,1)S(1)}, bf16[1,64,4096]{2,1,0:T(8,128)(2,1)S(1)}, u32[]{:S(2)}, u32[]{:S(2)}) collective-permute-start(bf16[1,64,4096]{2,1,0:T(8,128)(2,1)S(1)} %all_gather.13), channel_id=1, source_target_pairs={{4,0},{8,4},{12,8},{5,1},{9,5},{13,9},{6,2},{10,6},{14,10},{7,3},{... | collective-permute-start | bytes 1572872 | tf_op jit(solution)/shard_map/ppermute | solution.py:24
  230.8 16.0 %collective-permute-start.2 = (bf16[1,64,4096]{2,1,0:T(8,128)(2,1)S(1)}, bf16[1,64,4096]{2,1,0:T(8,128)(2,1)S(1)}, u32[]{:S(2)}, u32[]{:S(2)}) collective-permute-start(bf16[1,64,4096]{2,1,0:T(8,128)(2,1)S(1)} %all_gather.13), channel_id=1, source_target_pairs={{0,4},{4,8},{8,12},{1,5},{5,9},{9,13},{2,6},{6,10},{10,14},{3,7},{... | collective-permute-start | bytes 1572872 | tf_op jit(solution)/shard_map/ppermute | solution.py:23
  263.8 29.5 %copy-start.3 = (f32[1,16,4096]{2,1,0:T(8,128)S(1)}, f32[1,16,4096]{2,1,0:T(8,128)}, u32[]{:S(2)}) copy-start(f32[1,16,4096]{2,1,0:T(8,128)} %reduce-scatter.12.cloned.1.call-done) | copy-start | bytes 786436
  263.8 29.5 %copy-start.4 = (f32[1,16,4096]{2,1,0:T(8,128)S(1)}, f32[1,16,4096]{2,1,0:T(8,128)}, u32[]{:S(2)}) copy-start(f32[1,16,4096]{2,1,0:T(8,128)} %reduce-scatter.6.cloned.1.call-done) | copy-start | bytes 786436
  263.8 29.5 %copy-start.5 = (f32[1,16,4096]{2,1,0:T(8,128)S(1)}, f32[1,16,4096]{2,1,0:T(8,128)}, u32[]{:S(2)}) copy-start(f32[1,16,4096]{2,1,0:T(8,128)} %reduce-scatter.8.cloned.1.call-done) | copy-start | bytes 786436
Sparse Core Ops, SparseCore 0:
  78.0 23.0 reduce-scatter.5
  103.7 24.9 reduce-scatter.11
  196.5 25.2 reduce-scatter.7
  224.3 24.8 reduce-scatter.13
  266.9 26.2 reduce-scatter.9
where the time goes:
time: 304 us; the launch traced here: 303 us
  waiting for transfers between devices  91.2 us (30%)
  local copies, waits for them, and re-layouts  69.2 us (23%)
  starting transfers between devices  39.2 us (13%)
  other arithmetic  33.6 us (11%)
  blocking collectives  29.2 us (10%)
  matrix products  26.2 us (9%)
  between operations  14 us (5%)
    reduce_scatter x5, waiting for transfers between devices, col_sums(): return lax.psum_scatter(array, 'col', scatter_dimension=1, tiled=True)  50 us
    all_gather x4, blocking collectives, col_rows(): return lax.all_gather(array, 'col', axis=1, tiled=True)  29.2 us
    ppermute x4, waiting for transfers between devices, passed_along(): return lax.ppermute(block, axis, route)  20 us
    scatter-add x2, other arithmetic, forward(): window = jnp.zeros((3 * rows_dev, BLK * CONF), jnp.float32).at[window_ind...  16.7 us
    dot_general x2, matrix products, forward(): jnp.einsum('jkab,jbl->jkal', blocks, sources.reshape(rows_dev, BLK, CONF)...  16.2 us
    reshape x2, local copies, waits for them, and re-layouts, forward(): block_terms.reshape(-1, BLK * CONF)  15.8 us
    reshape x2, local copies, waits for them, and re-layouts, adjoint(): picked = window[window_index].reshape(rows_dev, slots_dev, BLK, CONF)  13.8 us
    ppermute x4, starting transfers between devices, passed_along(): return lax.ppermute(block, axis, route)  12.1 us
  transfers between devices with their start and end apart: 16, of which 12 were waited for; matrix products, arithmetic and copies ran while one was open for 33% of the time, Pallas kernels for 0%

commit v1 on v0

v1 whole, which is shorter than its diff:
```python
import functools

import jax
import jax.numpy as jnp
from jax import lax
from jax.experimental import pallas as pl
from jax.experimental.pallas import tpu as pltpu
from jax.sharding import PartitionSpec as P

BLK = 64
CONF = 64
PK = BLK * CONF // 128
MESH = pl.DeviceIdType.MESH
F32 = jnp.float32
BF16 = jnp.bfloat16
VMEM_BYTES = 50 * 1024 * 1024


class Net:
    def __init__(self, send_sems, recv_sems):
        self.send_sems, self.recv_sems, self.used = send_sems, recv_sems, 0

    def copy(self, src, dst, target):
        n = self.used
        self.used += 1
        return pltpu.make_async_remote_copy(
            src_ref=src,
            dst_ref=dst,
            send_sem=self.send_sems.at[n],
            recv_sem=self.recv_sems.at[n],
            device_id=target,
            device_id_type=MESH,
        )


def place():
    col = lax.axis_index("col")
    return lax.axis_index("space"), col // 2, col % 2


def greet(n_x, z_all, n_s):
    s, x, core = place()
    barrier = pltpu.get_barrier_semaphore()
    targets = [{"col": 2 * x + 1 - core}]
    targets += [{"col": 2 * ((x + d) % n_x) + core} for d in range(1, n_x)]
    if z_all:
        targets += [{"space": (s + d) % n_s} for d in range(1, n_s)]
    for target in targets:
        pl.semaphore_signal(barrier, inc=1, device_id=target, device_id_type=MESH)
    if not z_all:

        @pl.when(s > 0)
        def _():
            pl.semaphore_signal(barrier, inc=1, device_id={"space": s - 1}, device_id_type=MESH)

        @pl.when(s < n_s - 1)
        def _():
            pl.semaphore_signal(barrier, inc=1, device_id={"space": s + 1}, device_id_type=MESH)

    if z_all:
        pl.semaphore_wait(barrier, len(targets))
    else:
        sides = (s > 0).astype(jnp.int32) + (s < n_s - 1).astype(jnp.int32)
        pl.semaphore_wait(barrier, len(targets) + sides)


def low_half(rows):
    return lax.broadcasted_iota(jnp.int32, (rows, 128), 1) < 64


class GatherCol:
    def __init__(self, net, buf, n_x, size, base=0):
        s, x, core = place()
        self.net, self.buf, self.n_x, self.size, self.base = net, buf, n_x, size, base
        self.x, self.core = x, core
        mine = self.piece(core, x)
        self.across = []
        for d in range(1, n_x):
            self.across.append(net.copy(mine, mine, {"col": 2 * ((x + d) % n_x) + core}))
        self.beside = [net.copy(mine, mine, {"col": 2 * x + 1 - core})]
        for cp in self.across + self.beside:
            cp.start()

    def piece(self, core, x):
        return self.buf.at[pl.ds(self.base + (core * self.n_x + x) * self.size, self.size)]

    def arrive_across(self):
        for d, cp in enumerate(self.across, 1):
            cp.wait_recv()
            got = self.piece(self.core, (self.x + self.n_x - d) % self.n_x)
            on = self.net.copy(got, got, {"col": 2 * self.x + 1 - self.core})
            on.start()
            self.beside.append(on)

    def finish(self):
        for cp in self.beside:
            cp.wait_recv()
        for cp in self.beside + self.across:
            cp.wait_send()


class GatherWindow:
    def __init__(self, net, buf, n_x, size, n_s):
        self.net, self.buf, self.n_s = net, buf, n_s
        self.run = 2 * n_x * size
        self.group = n_x * size
        self.col = GatherCol(net, buf, n_x, size, self.run)

    def half(self, run, core):
        return self.buf.at[pl.ds(run * self.run + core * self.group, self.group)]

    def along(self):
        s, x, core = place()
        n_s, net = self.n_s, self.net
        self.col.arrive_across()
        self.up = net.copy(self.half(1, core), self.half(0, core), {"space": s + 1})
        self.down = net.copy(self.half(1, core), self.half(2, core), {"space": s - 1})
        pl.when(s < n_s - 1)(self.up.start)
        pl.when(s > 0)(self.down.start)

    def finish(self):
        s, x, core = place()
        n_s, net = self.n_s, self.net
        other = {"col": 2 * x + 1 - core}
        before = net.copy(self.half(0, core), self.half(0, core), other)
        after = net.copy(self.half(2, core), self.half(2, core), other)

        @pl.when(s > 0)
        def _():
            self.up.wait_recv()
            before.start()

        @pl.when(s < n_s - 1)
        def _():
            self.down.wait_recv()
            after.start()

        self.col.finish()

        @pl.when(s > 0)
        def _():
            before.wait_recv()
            before.wait_send()
            self.down.wait_send()

        @pl.when(s < n_s - 1)
        def _():
            after.wait_recv()
            after.wait_send()
            self.up.wait_send()


class SumForward:
    def __init__(self, net, part, got_core, z_out, z_in, x_out, x_in, n_x, size, n_s):
        s, x, core = place()
        self.net, self.part, self.got_core = net, part, got_core
        self.z_out, self.z_in, self.x_out, self.x_in = z_out, z_in, x_out, x_in
        self.n_x, self.size, self.n_s = n_x, size, n_s
        self.run, self.group = 2 * n_x * size, n_x * size
        group = self.group
        self.first = []
        for r in (0, 2, 1):
            src = part.at[pl.ds(r * self.run + (1 - core) * group, group)]
            cp = net.copy(src, got_core.at[pl.ds(r * group, group)], {"col": 2 * x + 1 - core})
            cp.start()
            self.first.append(cp)

    def pair(self, r, start, count):
        s, x, core = place()
        mine = self.part[pl.ds(r * self.run + core * self.group + start, count)]
        return mine.astype(F32) + self.got_core[pl.ds(r * self.group + start, count)].astype(F32)

    def along(self):
        s, x, core = place()
        group = self.group
        self.z = [
            self.net.copy(self.z_out.at[0], self.z_in.at[1], {"space": s - 1}),
            self.net.copy(self.z_out.at[1], self.z_in.at[0], {"space": s + 1}),
        ]
        self.first[0].wait_recv()

        @pl.when(s > 0)
        def _():
            self.z_out[0] = self.pair(0, 0, group).astype(BF16)
            self.z[0].start()

        self.first[1].wait_recv()

        @pl.when(s < self.n_s - 1)
        def _():
            self.z_out[1] = self.pair(2, 0, group).astype(BF16)
            self.z[1].start()

        @pl.when(s == 0)
        def _():
            self.z_in[0] = jnp.zeros(self.z_in.shape[1:], BF16)

        @pl.when(s == self.n_s - 1)
        def _():
            self.z_in[1] = jnp.zeros(self.z_in.shape[1:], BF16)

    def rows(self, at):
        start, count = at * self.size, self.size
        total = self.pair(1, start, count)
        for side in range(2):
            total = total + self.z_in[side, pl.ds(start, count)].astype(F32)
        return total

    def across(self):
        s, x, core = place()
        self.first[2].wait_recv()
        pl.when(s > 0)(self.z[1].wait_recv)
        pl.when(s < self.n_s - 1)(self.z[0].wait_recv)
        self.x = []
        for d in range(1, self.n_x):
            to = (x + d) % self.n_x
            self.x_out[d - 1] = self.rows(to).astype(BF16)
            cp = self.net.copy(self.x_out.at[d - 1], self.x_in.at[d - 1], {"col": 2 * to + core})
            cp.start()
            self.x.append(cp)

    def finish(self):
        s, x, core = place()
        total = self.rows(x)
        for d in range(1, self.n_x):
            self.x[d - 1].wait_recv()
            total = total + self.x_in[d - 1].astype(F32)
        for cp in self.first + self.x:
            cp.wait_send()
        pl.when(s > 0)(self.z[0].wait_send)
        pl.when(s < self.n_s - 1)(self.z[1].wait_send)
        return total


class SumCol:
    def __init__(self, net, part, got_core, x_out, x_in, n_x, size):
        s, x, core = place()
        self.net, self.part, self.got_core = net, part, got_core
        self.x_out, self.x_in, self.n_x, self.size = x_out, x_in, n_x, size
        self.group = n_x * size
        self.first = []
        for d in list(range(1, n_x)) + [0]:
            to = (x + d) % n_x
            src = part.at[pl.ds((1 - core) * self.group + to * size, size)]
            cp = net.copy(src, got_core.at[pl.ds(to * size, size)], {"col": 2 * x + 1 - core})
            cp.start()
            self.first.append(cp)

    def rows(self, at):
        s, x, core = place()
        mine = self.part[pl.ds(core * self.group + at * self.size, self.size)]
        return mine + self.got_core[pl.ds(at * self.size, self.size)]

    def across(self):
        s, x, core = place()
        self.x = []
        for d in range(1, self.n_x):
            to = (x + d) % self.n_x
            self.first[d - 1].wait_recv()
            self.x_out[d - 1] = self.rows(to)
            cp = self.net.copy(self.x_out.at[d - 1], self.x_in.at[d - 1], {"col": 2 * to + core})
            cp.start()
            self.x.append(cp)

    def finish(self):
        s, x, core = place()
        self.first[-1].wait_recv()
        total = self.rows(x)
        for d in range(1, self.n_x):
            self.x[d - 1].wait_recv()
            total = total + self.x_in[d - 1]
        for cp in self.first + self.x:
            cp.wait_send()
        return total


def start_kernel(
    n_x, n_s, emission, view, meta, form, rows_perm, lanes_perm,
    src, views, metas, fwd_form, adj_form, unpacked, send_sems, recv_sems, local_sem,
):
    s, x, core = place()
    size = emission.shape[0]
    cap = view.shape[1]
    net = Net(send_sems, recv_sems)
    where = core * n_x + x
    for i in range(PK):
        unpacked[:, i, :] = emission[:, i * 128 : (i + 1) * 128].astype(F32)
    src[pl.ds(where * size, size)] = unpacked[...].astype(BF16)
    at = where * n_s + s
    own_view = pltpu.make_async_copy(view.at[s], views.at[at], local_sem.at[0])
    own_view.start()
    own_meta = pltpu.make_async_copy(meta.at[s], metas.at[at], local_sem.at[1])
    own_meta.start()
    greet(n_x, True, n_s)
    spread = []
    for d in range(1, n_s):
        to = (s + d) % n_s
        spread.append(net.copy(view.at[to], views.at[at], {"space": to}))
        spread.append(net.copy(meta.at[to], metas.at[at], {"space": to}))
    for cp in spread:
        cp.start()
    gather = GatherCol(net, src, n_x, size)

    def prepare(j, carry):
        c, r = j // size, j % size
        to = ((c % 2) * n_x + c // 2) * size + r
        plain = jnp.dot(rows_perm[...], form[j], preferred_element_type=F32).astype(BF16)
        fwd_form[to] = jnp.dot(plain, lanes_perm[...], preferred_element_type=F32).astype(BF16)
        adj_form[to] = lax.dot_general(
            lanes_perm[...], plain, (((0,), (1,)), ((), ())), preferred_element_type=F32
        ).astype(BF16)
        return carry

    half = form.shape[0] // 2
    lax.fori_loop(0, half, prepare, 0)
    own_view.wait()
    own_meta.wait()
    for cp in spread:
        cp.wait_recv()
    gather.arrive_across()
    more = [GatherCol(net, views, n_x, n_s), GatherCol(net, metas, n_x, n_s)]
    lax.fori_loop(half, form.shape[0], prepare, 0)
    for g in more:
        g.arrive_across()
    gather.finish()
    for g in more:
        g.finish()
    for cp in spread:
        cp.wait_send()


def forward_step(j, form, src, index, slots, window):
    low = low_half(PK)
    piece = src[j].astype(F32)
    turned = pltpu.roll(piece, 64, 1)
    zero = jnp.zeros_like(piece)
    wide = jnp.concatenate(
        [
            jnp.where(low, piece, zero),
            jnp.where(low, turned, zero),
            jnp.where(low, zero, turned),
            jnp.where(low, zero, piece),
        ],
        axis=0,
    ).astype(BF16)
    terms = jnp.dot(form[j], wide, preferred_element_type=F32)
    for k in range(slots):
        at = index[j * slots + k]
        window[at] = window[at] + terms[k * PK : (k + 1) * PK]


def adjoint_step(j, form, vector, index, slots, out):
    low = low_half(PK)
    picked = jnp.concatenate([vector[index[j * slots + k]] for k in range(slots)], axis=0)
    m = jnp.dot(form[j], picked, preferred_element_type=F32)
    even = m[:PK] + pltpu.roll(m[2 * PK : 3 * PK], 64, 1)
    odd = pltpu.roll(m[PK : 2 * PK], 64, 1) + m[3 * PK :]
    out[j] = jnp.where(low, even, odd)


def loop(count, step, unroll):
    def body(t, carry):
        for u in range(unroll):
            step(t * unroll + u)
        return carry

    lax.fori_loop(0, count // unroll, body, 0)


def clear(window):
    def body(t, carry):
        window[pl.ds(t * 8, 8)] = jnp.zeros((8,) + window.shape[1:], F32)
        return carry

    lax.fori_loop(0, window.shape[0] // 8, body, 0)


def write_part(window, part):
    def body(t, carry):
        part[pl.ds(t * 8, 8)] = window[pl.ds(t * 8, 8)].astype(BF16)
        return carry

    lax.fori_loop(0, window.shape[0] // 8, body, 0)


def first_local(slots, n_x, index, metas, form, src, views, gain, part, view_total, scaled, window, lists):
    c = lax.axis_index("col")
    size = view_total.shape[0]
    clear(window)
    loop(form.shape[0], lambda j: forward_step(j, form, src, index, slots, window), 4)
    write_part(window, part)
    view_total[...] = jnp.zeros_like(view_total)
    cap = views.shape[1]

    def one_list(t, carry):
        for i in range(PK):
            lists[:, i, :] = views[t, :, i * 128 : (i + 1) * 128].astype(F32)
        for q in range(cap):
            at = metas[t, 0, q] - c * size

            @pl.when((at >= 0) & (at < size))
            def _():
                view_total[at] = view_total[at] + lists[q]

        return carry

    lax.fori_loop(0, views.shape[0], one_list, 0)
    scaled[...] = (gain[...] * view_total[...]).astype(BF16)


def middle_kernel(
    n_x, n_s, part, src, gain, scaled, first_sums, bounced, vector,
    got_core, z_out, z_in, x_out, x_in, send_sems, recv_sems,
):
    s, x, core = place()
    size = scaled.shape[0]
    net = Net(send_sems, recv_sems)
    greet(n_x, False, n_s)
    mine = (core * n_x + x) * size
    run = 2 * n_x * size
    sums = SumForward(net, part, got_core, z_out, z_in, x_out, x_in, n_x, size, n_s)
    vector[pl.ds(run + mine, size)] = scaled[...]
    gather = GatherWindow(net, vector, n_x, size, n_s)
    sums.along()
    sums.across()
    gather.along()
    total = sums.finish()
    first_sums[...] = total
    bounced[pl.ds(mine, size)] = (src[pl.ds(mine, size)].astype(F32) + gain[...] * total).astype(BF16)
    second = GatherCol(net, bounced, n_x, size)
    second.arrive_across()
    gather.finish()
    second.finish()


def second_local(slots, index, fwd_form, adj_form, src, vector, part, adjoint, window):
    clear(window)

    def step(j):
        forward_step(j, fwd_form, src, index, slots, window)
        adjoint_step(j, adj_form, vector, index, slots, adjoint)

    loop(fwd_form.shape[0], step, 2)
    write_part(window, part)


def end_kernel(
    slots, n_x, n_s, index, part, adjoint, adj_form, first_sums, view_total, gain,
    grad_emission, grad_reflect,
    vector, last, keep, got_core, z_out, z_in, x_out, x_in,
    one_core, one_out, one_in, two_core, two_out, two_in, send_sems, recv_sems,
):
    s, x, core = place()
    size = view_total.shape[0]
    net = Net(send_sems, recv_sems)
    greet(n_x, False, n_s)
    mine = (core * n_x + x) * size
    run = 2 * n_x * size
    one = SumCol(net, adjoint, one_core, one_out, one_in, n_x, size)
    one.across()
    sums = SumForward(net, part, got_core, z_out, z_in, x_out, x_in, n_x, size, n_s)
    sums.along()
    adjoint_one = one.finish()
    vector[pl.ds(run + mine, size)] = (gain[...] * adjoint_one).astype(BF16)
    keep[...] = adjoint_one
    gather = GatherWindow(net, vector, n_x, size, n_s)
    gather.along()
    sums.across()
    gather.finish()
    loop(adj_form.shape[0], lambda j: adjoint_step(j, adj_form, vector, index, slots, last), 4)
    two = SumCol(net, last, two_core, two_out, two_in, n_x, size)
    two.across()
    second_sums = sums.finish()
    product = view_total[...] * second_sums + keep[...] * first_sums[...]
    low = lax.broadcasted_iota(jnp.int32, product.shape, 2) < 64
    grad_reflect[0] = jnp.sum(jnp.where(low, product, 0.0), axis=2)
    grad_reflect[1] = jnp.sum(jnp.where(low, 0.0, product), axis=2)
    keep[...] = view_total[...] + keep[...] + two.finish()
    for i in range(PK):
        grad_emission[:, i * 128 : (i + 1) * 128] = keep[:, i, :]


def call(kernel, outs, scratch, operands, smem=0, remote=None):
    vmem = pl.BlockSpec(memory_space=pltpu.VMEM)
    specs = [pl.BlockSpec(memory_space=pltpu.SMEM)] * smem + [vmem] * (len(operands) - smem)
    if remote is None:
        params = pltpu.CompilerParams(vmem_limit_bytes=VMEM_BYTES)
    else:
        params = pltpu.CompilerParams(
            vmem_limit_bytes=VMEM_BYTES, collective_id=remote, has_side_effects=True
        )
    return pl.pallas_call(
        kernel,
        out_shape=[jax.ShapeDtypeStruct(*out) for out in outs],
        in_specs=specs,
        out_specs=[vmem] * len(outs),
        scratch_shapes=scratch,
        compiler_params=params,
    )(*operands)


def body(n_s, n_c, emission, reflect, form_blocks, block_rows, view_grads, view_rows, view_counts):
    n_x = n_c // 2
    rows, slots = form_blocks.shape[0], form_blocks.shape[2]
    size = emission.shape[0]
    cap = view_grads.shape[3]
    s = lax.axis_index("space")
    tall = slots * PK
    form = form_blocks.reshape(rows, slots, PK, 128).transpose(0, 2, 1, 3).reshape(rows, tall, 128)
    a, b = jnp.arange(tall)[:, None], jnp.arange(tall)[None, :]
    rows_perm = ((a % PK) * slots + a // PK == b).astype(BF16)
    q, p = jnp.arange(128)[:, None], jnp.arange(128)[None, :]
    lanes_perm = (q == (p // 64) * 64 + 2 * (p % 32) + (p % 64) // 32).astype(BF16)
    target = block_rows.reshape(rows, slots) - (s - 1) * rows
    block = target % rows
    piece = block // size
    target = target - block + ((piece % 2) * n_x + piece // 2) * size + block % size
    index = target.reshape(n_x, 2, size, slots).transpose(1, 0, 2, 3).reshape(rows * slots)
    live = jnp.arange(cap, dtype=jnp.int32) < view_counts[0, 0][:, None]
    meta = jnp.where(live, view_rows[0, 0], -1)
    meta = jnp.pad(meta, ((0, 0), (0, 128 - cap)))[:, None, :]
    gain = jnp.broadcast_to(reflect.reshape(size, PK, 2, 1), (size, PK, 2, 64)).reshape(size, PK, 128)

    dma = pltpu.SemaphoreType.DMA
    blocks = lambda n: (n, PK, 128)
    src, views, metas, fwd_form, adj_form = call(
        functools.partial(start_kernel, n_x, n_s),
        [
            (blocks(rows), BF16),
            ((n_c * n_s, cap, BLK * CONF), BF16),
            ((n_c * n_s, 1, 128), jnp.int32),
            ((rows, tall, 128), BF16),
            ((rows, 128, tall), BF16),
        ],
        [pltpu.VMEM(blocks(size), F32)] + [dma((2 * n_s + 6 * n_x,))] * 2 + [dma((2,))],
        (emission, view_grads[0, 0], meta, form, rows_perm, lanes_perm),
        remote=0,
    )
    part_one, view_total, scaled_one = call(
        functools.partial(first_local, slots, n_x),
        [(blocks(3 * rows), BF16), (blocks(size), F32), (blocks(size), BF16)],
        [pltpu.VMEM(blocks(3 * rows), F32), pltpu.VMEM(blocks(cap), F32)],
        (index, metas, fwd_form, src, views, gain),
        smem=2,
    )
    group = n_x * size
    sum_bufs = [
        pltpu.VMEM(blocks(3 * group), BF16),
        pltpu.VMEM((2,) + blocks(group), BF16),
        pltpu.VMEM((2,) + blocks(group), BF16),
        pltpu.VMEM((n_x - 1,) + blocks(size), BF16),
        pltpu.VMEM((n_x - 1,) + blocks(size), BF16),
    ]
    first_sums, bounced, vector = call(
        functools.partial(middle_kernel, n_x, n_s),
        [(blocks(size), F32), (blocks(rows), BF16), (blocks(3 * rows), BF16)],
        sum_bufs + [dma((9 + 5 * n_x,))] * 2,
        (part_one, src, gain, scaled_one),
        remote=1,
    )
    part_two, adjoint_one = call(
        functools.partial(second_local, slots),
        [(blocks(3 * rows), BF16), (blocks(rows), F32)],
        [pltpu.VMEM(blocks(3 * rows), F32)],
        (index, fwd_form, adj_form, bounced, vector),
        smem=1,
    )
    col_bufs = [
        pltpu.VMEM(blocks(group), F32),
        pltpu.VMEM((n_x - 1,) + blocks(size), F32),
        pltpu.VMEM((n_x - 1,) + blocks(size), F32),
    ]
    grad_emission, grad_reflect = call(
        functools.partial(end_kernel, slots, n_x, n_s),
        [((size, BLK * CONF), F32), ((2, size, PK), F32)],
        [pltpu.VMEM(blocks(3 * rows), BF16), pltpu.VMEM(blocks(rows), F32), pltpu.VMEM(blocks(size), F32)]
        + sum_bufs + col_bufs * 2 + [dma((9 + 8 * n_x,))] * 2,
        (index, part_two, adjoint_one, adj_form, first_sums, view_total, gain),
        smem=1,
        remote=2,
    )
    return grad_emission, grad_reflect.transpose(1, 2, 0).reshape(size * BLK)


def solution(mesh):
    in_specs = (
        P(("level", "space", "col"), None),
        P(("level", "space", "col")),
        P(("level", "space"), "col", None, None),
        P(("level", "space"), "col", None),
        P(("level", "space"), "col", None, None, None),
        P(("level", "space"), "col", None, None),
        P(("level", "space"), "col", None),
    )
    out_specs = (P(("level", "space", "col"), None), P(("level", "space", "col")))
    step = functools.partial(body, mesh.shape["space"], mesh.shape["col"])
    return jax.shard_map(step, mesh=mesh, in_specs=in_specs, out_specs=out_specs, check_vma=False)
```

time: 304 us -> 119 us (0.39)
  Pallas kernels: 0 us -> 109 us
  waiting for transfers between devices: 91.2 us -> 0 us
  local copies, waits for them, and re-layouts: 69.2 us -> 7.38 us
  starting transfers between devices: 39.2 us -> 0 us
  other arithmetic: 33.6 us -> 1.7 us
  blocking collectives: 29.2 us -> 0 us
  matrix products: 26.2 us -> 0 us
  between operations: 14 us -> 0.77 us
    pallas_call x0 -> x5, Pallas kernels: none -> 109 us  [call(): pl.pallas_call(kernel, out_shape=[jax.ShapeDtypeStruct(*out) for out in o...]
    reduce_scatter x5 -> x0, waiting for transfers between devices: 50 us -> none  [col_sums(): return lax.psum_scatter(array, 'col', scatter_dimension=1, tiled=True)]
    reshape x10 -> x3, local copies, waits for them, and re-layouts: 41.7 us -> 1.16 us  [the longest x1 0.76 us: body(): return (grad_emission, grad_reflect.transpose(1, 2, 0).reshape(size * BLK))]
    ppermute x8 -> x0, waiting for transfers between devices: 31.3 us -> none  [the longest x4 20 us: passed_along(): return lax.ppermute(block, axis, route)]
    all_gather x4 -> x0, blocking collectives: 29.2 us -> none  [col_rows(): return lax.all_gather(array, 'col', axis=1, tiled=True)]
    dot_general x4 -> x0, matrix products: 26.2 us -> none  [the longest x2 16.2 us: forward(): jnp.einsum('jkab,jbl->jkal', blocks, sources.reshape(rows_dev, BLK, CONF)...]
    ppermute x8 -> x0, starting transfers between devices: 24.6 us -> none  [the longest x4 12.1 us: passed_along(): return lax.ppermute(block, axis, route)]
    scatter-add x3 -> x0, other arithmetic: 19.1 us -> none  [the longest x2 16.7 us: forward(): window = jnp.zeros((3 * rows_dev, BLK * CONF), jnp.float32).at[window_ind...]
  transfers between devices with their start and end apart: 16 -> 0, of which waited for: 12 -> 0; matrix products, arithmetic and copies ran while one was open for 33% -> 0% of each run, Pallas kernels for 0% -> 0%
where the time goes in v1:
time: 119 us
  Pallas kernels  109 us (92%)
  local copies, waits for them, and re-layouts  7.38 us (6%)
  other arithmetic  1.7 us (1%)
    pallas_call x5, Pallas kernels, call(): pl.pallas_call(kernel, out_shape=[jax.ShapeDtypeStruct(*out) for out in o...  109 us
    unnamed x11, local copies, waits for them, and re-layouts  4.36 us

profile of v1, /device:TPU:0, one launch (start us, length us, event | category | flops | bytes accessed | tf_op | source)
XLA Modules:
  0.0 118.6 jit_solution(4105594565394801065)
XLA Ops:
  0.6 0.0 copy-start.4
  0.6 0.0 copy-start.3
  0.7 0.8 broadcast_subtract_fusion
  1.4 0.8 bitcast_select_fusion
  2.2 0.1 sub.46
  2.3 0.1 copy.13
  2.4 0.1 fusion.8
  2.5 0.1 reshape.188.index
  2.6 0.1 fusion
  2.7 0.9 broadcast_in_dim.21
  3.6 0.6 broadcast_in_dim.22
  4.2 0.3 reshape.191.gain
  4.5 0.0 copy-done.4
  4.5 0.0 copy-done.3
  4.5 28.8 %shard_map.86 = (bf16[64,32,128]{2,1,0:T(8,128)(2,1)S(1)}, bf16[16,4,4096]{2,1,0:T(4,128)(2,1)S(1)}, s32[16,1,128]{2,1,0:T(1,128)S(1)}, bf16[64,128,128]{2,1,0:T(8,128)(2,1)S(1)}, bf16[64,128,128]{2,1,0:T(8,128)(2,1)}) custom-call(bf16[16,4096]{1,0:T(8,128)(2,1)S(1)} %copy-done.3, bf16[4,4,4096]{2,1,0:T(4,128)(2,1)S(1)} %bitcast.17, ...), custom_call_target="tpu_custom_call" | custom-call | tf_op jit(solution)/shard_map/pallas_call | solution.py:492
  33.3 0.0 copy-start
  33.3 1.3 %copy-done = bf16[64,128,128]{2,1,0:T(8,128)(2,1)} copy-done((bf16[64,128,128]{2,1,0:T(8,128)(2,1)}, bf16[64,128,128]{2,1,0:T(8,128)(2,1)S(1)}, u32[]{:S(2)}) %copy-start) | copy-done | bytes 2097176
  34.6 7.9 %shard_map.87 = (bf16[192,32,128]{2,1,0:T(8,128)(2,1)S(1)}, f32[16,32,128]{2,1,0:T(8,128)S(1)}, bf16[16,32,128]{2,1,0:T(8,128)(2,1)S(1)}) custom-call(s32[256]{0:T(256)S(1)} %reshape.188.index, s32[16,1,128]{2,1,0:T(1,128)S(1)} %get-tuple-element.19.metas, bf16[64,128,128]{2,1,0:T(8,128)(2,1)} %copy-done, bf16[64,32,128]{2,1,0:T(8,128)(2,1)S(1)} %get-tuple-element.20.src, ...), custom_call_target="tpu_custom_call" | custom-call | tf_op jit(solution)/shard_map/pallas_call | solution.py:492
  42.5 0.0 copy-start.1
  42.5 1.2 copy-done.1
  43.7 21.9 %shard_map.88 = (f32[16,32,128]{2,1,0:T(8,128)S(1)}, bf16[64,32,128]{2,1,0:T(8,128)(2,1)S(1)}, bf16[192,32,128]{2,1,0:T(8,128)(2,1)S(1)}) custom-call(bf16[192,32,128]{2,1,0:T(8,128)(2,1)} %copy-done.1, bf16[64,32,128]{2,1,0:T(8,128)(2,1)S(1)} %get-tuple-element.20.src, f32[16,32,128]{2,1,0:T(8,128)S(1)} %reshape.191.gain, ...), custom_call_target="tpu_custom_call" | custom-call | tf_op jit(solution)/shard_map/pallas_call | solution.py:492
  65.6 0.0 copy-start.2
  65.6 1.2 copy-done.2
  66.8 10.9 %shard_map.89 = (bf16[192,32,128]{2,1,0:T(8,128)(2,1)S(1)}, f32[64,32,128]{2,1,0:T(8,128)S(1)}) custom-call(s32[256]{0:T(256)S(1)} %reshape.188.index, bf16[64,128,128]{2,1,0:T(8,128)(2,1)} %copy-done, bf16[64,128,128]{2,1,0:T(8,128)(2,1)} %get-tuple-element.18.adj_form, bf16[64,32,128]{2,1,0:T(8,128)(2,1)S(1)} %get-tuple-element.24.src, ...), custom_call_target="tpu_custom_call" | custom-call | tf_op jit(solution)/shard_map/pallas_call | solution.py:492
  77.7 39.2 %shard_map.90 = (f32[16,4096]{1,0:T(8,128)S(1)}, f32[2,16,32]{2,1,0:T(8,128)S(1)}) custom-call(s32[256]{0:T(256)S(1)} %reshape.188.index, bf16[192,32,128]{2,1,0:T(8,128)(2,1)S(1)} %get-tuple-element.26.part, f32[64,32,128]{2,1,0:T(8,128)S(1)} %get-tuple-element.27.adjoint, bf16[64,128,128]{2,1,0:T(8,128)(2,1)} %get-tuple-element.18.adj_form, ...), custom_call_target="tpu_custom_call" | custom-call | tf_op jit(solution)/shard_map/pallas_call | solution.py:492
  116.9 0.2 copy.15
  117.1 0.8 reshape.192
  117.9 0.7 copy.17
  (3 shorter events, 0.0 us)
Async XLA Ops:
  0.6 3.9 %copy-start.4 = (bf16[1,1,4,4,4096]{4,3,2,1,0:T(4,128)(2,1)S(1)}, bf16[1,1,4,4,4096]{4,3,2,1,0:T(4,128)(2,1)}, u32[]{:S(2)}) copy-start(bf16[1,1,4,4,4096]{4,3,2,1,0:T(4,128)(2,1)} %param.11) | copy-start | bytes 393220
  0.6 3.9 %copy-start.3 = (bf16[16,4096]{1,0:T(8,128)(2,1)S(1)}, bf16[16,4096]{1,0:T(8,128)(2,1)}, u32[]{:S(2)}) copy-start(bf16[16,4096]{1,0:T(8,128)(2,1)} %emission.1) | copy-start | bytes 393220
  33.3 1.3 %copy-start = (bf16[64,128,128]{2,1,0:T(8,128)(2,1)}, bf16[64,128,128]{2,1,0:T(8,128)(2,1)S(1)}, u32[]{:S(2)}) copy-start(bf16[64,128,128]{2,1,0:T(8,128)(2,1)S(1)} %get-tuple-element.17.form.fwd_form) | copy-start | bytes 6291460
  42.5 1.2 copy-start.1
  65.6 1.2 copy-start.2

commit v2 on v1

--- a/solution.py
+++ b/solution.py
@@ -13,7 +13,7 @@
 MESH = pl.DeviceIdType.MESH
 F32 = jnp.float32
 BF16 = jnp.bfloat16
-VMEM_BYTES = 50 * 1024 * 1024
+VMEM_BYTES = 32 * 1024 * 1024
 
 
 class Net:
@@ -214,7 +214,7 @@
         self.x = []
         for d in range(1, self.n_x):
             to = (x + d) % self.n_x
-            self.x_out[d - 1] = self.rows(to).astype(BF16)
+            self.x_out[d - 1] = self.rows(to)
             cp = self.net.copy(self.x_out.at[d - 1], self.x_in.at[d - 1], {"col": 2 * to + core})
             cp.start()
             self.x.append(cp)
@@ -224,7 +224,7 @@
         total = self.rows(x)
         for d in range(1, self.n_x):
             self.x[d - 1].wait_recv()
-            total = total + self.x_in[d - 1].astype(F32)
+            total = total + self.x_in[d - 1]
         for cp in self.first + self.x:
             cp.wait_send()
         pl.when(s > 0)(self.z[0].wait_send)
@@ -274,13 +274,24 @@
         return total
 
 
+def patch_masks(p):
+    i = lax.broadcasted_iota(jnp.int32, (PK, 128), 0)
+    t = lax.broadcasted_iota(jnp.int32, (PK, 128), 1)
+    rows = t == (p % 2) * 64 + 2 * i + t % 2
+    patch = lax.broadcasted_iota(jnp.int32, (128, 128), 0)
+    lane = lax.broadcasted_iota(jnp.int32, (128, 128), 1)
+    return rows, (patch % 2 == lane // 64).astype(F32)
+
+
 def start_kernel(
-    n_x, n_s, emission, view, meta, form, rows_perm, lanes_perm,
-    src, views, metas, fwd_form, adj_form, unpacked, send_sems, recv_sems, local_sem,
+    n_x, n_s, emission, reflect, view, meta, form, rows_perm, lanes_perm,
+    src, fwd_form, adj_form, gain, view_total, vector,
+    views, metas, entries, unpacked, send_sems, recv_sems, local_sem,
 ):
     s, x, core = place()
     size = emission.shape[0]
     cap = view.shape[1]
+    rows = form.shape[0]
     net = Net(send_sems, recv_sems)
     where = core * n_x + x
     for i in range(PK):
@@ -301,7 +312,7 @@
         cp.start()
     gather = GatherCol(net, src, n_x, size)
 
-    def prepare(j, carry):
+    def prepare(j):
         c, r = j // size, j % size
         to = ((c % 2) * n_x + c // 2) * size + r
         plain = jnp.dot(rows_perm[...], form[j], preferred_element_type=F32).astype(BF16)
@@ -309,22 +320,43 @@
         adj_form[to] = lax.dot_general(
             lanes_perm[...], plain, (((0,), (1,)), ((), ())), preferred_element_type=F32
         ).astype(BF16)
-        return carry
-
-    half = form.shape[0] // 2
-    lax.fori_loop(0, half, prepare, 0)
+
+    loop(0, rows // 4, prepare, 8)
+    for p in range(size):
+        sel, lanes = patch_masks(p)
+        picked = jnp.where(sel, reflect[p // 2 : p // 2 + 1, :], 0.0)
+        gain[p] = jnp.dot(
+            picked, lanes, preferred_element_type=F32, precision=lax.Precision.HIGHEST
+        )
     own_view.wait()
     own_meta.wait()
     for cp in spread:
         cp.wait_recv()
+    more = [GatherCol(net, views, n_x, n_s), GatherCol(net, metas, n_x, n_s)]
     gather.arrive_across()
-    more = [GatherCol(net, views, n_x, n_s), GatherCol(net, metas, n_x, n_s)]
-    lax.fori_loop(half, form.shape[0], prepare, 0)
+    loop(rows // 4, rows // 4, prepare, 8)
     for g in more:
         g.arrive_across()
     gather.finish()
     for g in more:
         g.finish()
+    count = views.shape[0] * cap
+    for t in range(views.shape[0]):
+        entries[t * cap : (t + 1) * cap, :] = views[t].astype(F32)
+    marks = jnp.sum(metas[...], axis=0)
+    wanted = lax.broadcasted_iota(jnp.int32, (size, marks.shape[1]), 0) + (2 * x + core) * size + 1
+    chosen = (wanted == marks).astype(F32).astype(BF16)[:, :count]
+    for i in range(0, PK, 4):
+        cut = entries[:, i * 128 : (i + 4) * 128].astype(BF16)
+        found = jnp.dot(chosen, cut, preferred_element_type=F32)
+        for u in range(4):
+            view_total[:, i + u, :] = found[:, u * 128 : (u + 1) * 128]
+    vector[pl.ds(2 * n_x * size + where * size, size)] = (gain[...] * view_total[...]).astype(BF16)
+    window = GatherWindow(net, vector, n_x, size, n_s)
+    loop(rows // 2, rows // 4, prepare, 8)
+    window.along()
+    loop(rows // 2 + rows // 4, rows // 4, prepare, 8)
+    window.finish()
     for cp in spread:
         cp.wait_send()
 
@@ -358,10 +390,10 @@
     out[j] = jnp.where(low, even, odd)
 
 
-def loop(count, step, unroll):
+def loop(first, count, step, unroll):
     def body(t, carry):
         for u in range(unroll):
-            step(t * unroll + u)
+            step(first + t * unroll + u)
         return carry
 
     lax.fori_loop(0, count // unroll, body, 0)
@@ -383,101 +415,81 @@
     lax.fori_loop(0, window.shape[0] // 8, body, 0)
 
 
-def first_local(slots, n_x, index, metas, form, src, views, gain, part, view_total, scaled, window, lists):
-    c = lax.axis_index("col")
-    size = view_total.shape[0]
+def forward_local(slots, index, form, src, part, window):
     clear(window)
-    loop(form.shape[0], lambda j: forward_step(j, form, src, index, slots, window), 4)
+    loop(0, form.shape[0], lambda j: forward_step(j, form, src, index, slots, window), 8)
     write_part(window, part)
-    view_total[...] = jnp.zeros_like(view_total)
-    cap = views.shape[1]
-
-    def one_list(t, carry):
-        for i in range(PK):
-            lists[:, i, :] = views[t, :, i * 128 : (i + 1) * 128].astype(F32)
-        for q in range(cap):
-            at = metas[t, 0, q] - c * size
-
-            @pl.when((at >= 0) & (at < size))
-            def _():
-                view_total[at] = view_total[at] + lists[q]
-
-        return carry
-
-    lax.fori_loop(0, views.shape[0], one_list, 0)
-    scaled[...] = (gain[...] * view_total[...]).astype(BF16)
 
 
 def middle_kernel(
-    n_x, n_s, part, src, gain, scaled, first_sums, bounced, vector,
-    got_core, z_out, z_in, x_out, x_in, send_sems, recv_sems,
+    slots, n_x, n_s, index, part, src, gain, vector, adj_form,
+    first_sums, bounced, adjoint_one, next_vector,
+    got_core, z_out, z_in, x_out, x_in,
+    terms, one_core, one_out, one_in, send_sems, recv_sems,
 ):
     s, x, core = place()
-    size = scaled.shape[0]
+    size = gain.shape[0]
     net = Net(send_sems, recv_sems)
     greet(n_x, False, n_s)
     mine = (core * n_x + x) * size
-    run = 2 * n_x * size
+    group = n_x * size
+    step = lambda j: adjoint_step(j, adj_form, vector, index, slots, terms)
     sums = SumForward(net, part, got_core, z_out, z_in, x_out, x_in, n_x, size, n_s)
-    vector[pl.ds(run + mine, size)] = scaled[...]
-    gather = GatherWindow(net, vector, n_x, size, n_s)
+    loop((1 - core) * group, group, step, 8)
+    one = SumCol(net, terms, one_core, one_out, one_in, n_x, size)
     sums.along()
+    loop(core * group, group, step, 8)
+    one.across()
     sums.across()
+    adjoint_one[...] = one.finish()
+    next_vector[pl.ds(2 * group + mine, size)] = (gain[...] * adjoint_one[...]).astype(BF16)
+    gather = GatherWindow(net, next_vector, n_x, size, n_s)
+    first_sums[...] = sums.finish()
+    bounced[pl.ds(mine, size)] = (
+        src[pl.ds(mine, size)].astype(F32) + gain[...] * first_sums[...]
+    ).astype(BF16)
+    second = GatherCol(net, bounced, n_x, size)
     gather.along()
-    total = sums.finish()
-    first_sums[...] = total
-    bounced[pl.ds(mine, size)] = (src[pl.ds(mine, size)].astype(F32) + gain[...] * total).astype(BF16)
-    second = GatherCol(net, bounced, n_x, size)
     second.arrive_across()
     gather.finish()
     second.finish()
 
 
-def second_local(slots, index, fwd_form, adj_form, src, vector, part, adjoint, window):
-    clear(window)
-
-    def step(j):
-        forward_step(j, fwd_form, src, index, slots, window)
-        adjoint_step(j, adj_form, vector, index, slots, adjoint)
-
-    loop(fwd_form.shape[0], step, 2)
-    write_part(window, part)
-
-
 def end_kernel(
-    slots, n_x, n_s, index, part, adjoint, adj_form, first_sums, view_total, gain,
+    slots, n_x, n_s, index, part, vector, adj_form, first_sums, adjoint_one, view_total,
     grad_emission, grad_reflect,
-    vector, last, keep, got_core, z_out, z_in, x_out, x_in,
-    one_core, one_out, one_in, two_core, two_out, two_in, send_sems, recv_sems,
+    got_core, z_out, z_in, x_out, x_in,
+    terms, two_core, two_out, two_in, send_sems, recv_sems,
 ):
     s, x, core = place()
     size = view_total.shape[0]
     net = Net(send_sems, recv_sems)
     greet(n_x, False, n_s)
-    mine = (core * n_x + x) * size
-    run = 2 * n_x * size
-    one = SumCol(net, adjoint, one_core, one_out, one_in, n_x, size)
-    one.across()
+    group = n_x * size
+    step = lambda j: adjoint_step(j, adj_form, vector, index, slots, terms)
     sums = SumForward(net, part, got_core, z_out, z_in, x_out, x_in, n_x, size, n_s)
+    loop((1 - core) * group, group, step, 8)
+    two = SumCol(net, terms, two_core, two_out, two_in, n_x, size)
     sums.along()
-    adjoint_one = one.finish()
-    vector[pl.ds(run + mine, size)] = (gain[...] * adjoint_one).astype(BF16)
-    keep[...] = adjoint_one
-    gather = GatherWindow(net, vector, n_x, size, n_s)
-    gather.along()
+    loop(core * group, group, step, 8)
+    two.across()
     sums.across()
-    gather.finish()
-    loop(adj_form.shape[0], lambda j: adjoint_step(j, adj_form, vector, index, slots, last), 4)
-    two = SumCol(net, last, two_core, two_out, two_in, n_x, size)
-    two.across()
-    second_sums = sums.finish()
-    product = view_total[...] * second_sums + keep[...] * first_sums[...]
-    low = lax.broadcasted_iota(jnp.int32, product.shape, 2) < 64
-    grad_reflect[0] = jnp.sum(jnp.where(low, product, 0.0), axis=2)
-    grad_reflect[1] = jnp.sum(jnp.where(low, 0.0, product), axis=2)
-    keep[...] = view_total[...] + keep[...] + two.finish()
+    got_two = two.finish()
+    keep = two_core
+    keep[pl.ds(0, size)] = view_total[...] + adjoint_one[...] + got_two
     for i in range(PK):
-        grad_emission[:, i * 128 : (i + 1) * 128] = keep[:, i, :]
+        grad_emission[:, i * 128 : (i + 1) * 128] = keep[:size, i, :]
+    keep[pl.ds(0, size)] = view_total[...] * sums.finish() + adjoint_one[...] * first_sums[...]
+    for p in range(0, size, 2):
+        total = jnp.zeros((1, 128), F32)
+        for q in (p, p + 1):
+            sel, lanes = patch_masks(q)
+            spread = lax.dot_general(
+                keep[q], lanes, (((1,), (1,)), ((), ())),
+                preferred_element_type=F32, precision=lax.Precision.HIGHEST,
+            )
+            total = total + jnp.sum(jnp.where(sel, spread, 0.0), axis=0, keepdims=True)
+        grad_reflect[p // 2 : p // 2 + 1, :] = total
 
 
 def call(kernel, outs, scratch, operands, smem=0, remote=None):
@@ -516,70 +528,81 @@
     piece = block // size
     target = target - block + ((piece % 2) * n_x + piece // 2) * size + block % size
     index = target.reshape(n_x, 2, size, slots).transpose(1, 0, 2, 3).reshape(rows * slots)
+    col = lax.axis_index("col")
+    lists = n_c * n_s
+    at = ((col % 2) * n_x + col // 2) * n_s + s
     live = jnp.arange(cap, dtype=jnp.int32) < view_counts[0, 0][:, None]
-    meta = jnp.where(live, view_rows[0, 0], -1)
-    meta = jnp.pad(meta, ((0, 0), (0, 128 - cap)))[:, None, :]
-    gain = jnp.broadcast_to(reflect.reshape(size, PK, 2, 1), (size, PK, 2, 64)).reshape(size, PK, 128)
+    marks = jnp.where(live, view_rows[0, 0] + 1, 0)[:, None, :]
+    own_list = jnp.arange(lists, dtype=jnp.int32)[None, :, None] == at
+    meta = jnp.where(own_list, marks, 0).reshape(n_s, lists * cap)
+    meta = jnp.pad(meta, ((0, 0), (0, -(lists * cap) % 128)))[:, None, :]
 
     dma = pltpu.SemaphoreType.DMA
     blocks = lambda n: (n, PK, 128)
-    src, views, metas, fwd_form, adj_form = call(
+    src, fwd_form, adj_form, gain, view_total, vector = call(
         functools.partial(start_kernel, n_x, n_s),
         [
             (blocks(rows), BF16),
-            ((n_c * n_s, cap, BLK * CONF), BF16),
-            ((n_c * n_s, 1, 128), jnp.int32),
             ((rows, tall, 128), BF16),
             ((rows, 128, tall), BF16),
+            (blocks(size), F32),
+            (blocks(size), F32),
+            (blocks(3 * rows), BF16),
         ],
-        [pltpu.VMEM(blocks(size), F32)] + [dma((2 * n_s + 6 * n_x,))] * 2 + [dma((2,))],
-        (emission, view_grads[0, 0], meta, form, rows_perm, lanes_perm),
+        [
+            pltpu.VMEM((lists, cap, BLK * CONF), BF16),
+            pltpu.VMEM((lists,) + meta.shape[1:], jnp.int32),
+            pltpu.VMEM((lists * cap, BLK * CONF), F32),
+            pltpu.VMEM(blocks(size), F32),
+        ]
+        + [dma((4 + 2 * n_s + 8 * n_x,))] * 2 + [dma((2,))],
+        (emission, reflect.reshape(-1, 128), view_grads[0, 0], meta, form, rows_perm, lanes_perm),
         remote=0,
     )
-    part_one, view_total, scaled_one = call(
-        functools.partial(first_local, slots, n_x),
-        [(blocks(3 * rows), BF16), (blocks(size), F32), (blocks(size), BF16)],
-        [pltpu.VMEM(blocks(3 * rows), F32), pltpu.VMEM(blocks(cap), F32)],
-        (index, metas, fwd_form, src, views, gain),
-        smem=2,
-    )
     group = n_x * size
-    sum_bufs = [
+
+    def forward(sources):
+        return call(
+            functools.partial(forward_local, slots),
+            [(blocks(3 * rows), BF16)],
+            [pltpu.VMEM(blocks(3 * rows), F32)],
+            (index, fwd_form, sources),
+            smem=1,
+        )[0]
+
+    bufs = [
         pltpu.VMEM(blocks(3 * group), BF16),
         pltpu.VMEM((2,) + blocks(group), BF16),
         pltpu.VMEM((2,) + blocks(group), BF16),
-        pltpu.VMEM((n_x - 1,) + blocks(size), BF16),
-        pltpu.VMEM((n_x - 1,) + blocks(size), BF16),
-    ]
-    first_sums, bounced, vector = call(
-        functools.partial(middle_kernel, n_x, n_s),
-        [(blocks(size), F32), (blocks(rows), BF16), (blocks(3 * rows), BF16)],
-        sum_bufs + [dma((9 + 5 * n_x,))] * 2,
-        (part_one, src, gain, scaled_one),
-        remote=1,
-    )
-    part_two, adjoint_one = call(
-        functools.partial(second_local, slots),
-        [(blocks(3 * rows), BF16), (blocks(rows), F32)],
-        [pltpu.VMEM(blocks(3 * rows), F32)],
-        (index, fwd_form, adj_form, bounced, vector),
-        smem=1,
-    )
-    col_bufs = [
+        pltpu.VMEM((n_x - 1,) + blocks(size), F32),
+        pltpu.VMEM((n_x - 1,) + blocks(size), F32),
+        pltpu.VMEM(blocks(rows), F32),
         pltpu.VMEM(blocks(group), F32),
         pltpu.VMEM((n_x - 1,) + blocks(size), F32),
         pltpu.VMEM((n_x - 1,) + blocks(size), F32),
     ]
+    first_sums, bounced, adjoint_one, next_vector = call(
+        functools.partial(middle_kernel, slots, n_x, n_s),
+        [
+            (blocks(size), F32),
+            (blocks(rows), BF16),
+            (blocks(size), F32),
+            (blocks(3 * rows), BF16),
+        ],
+        bufs + [dma((9 + 8 * n_x,))] * 2,
+        (index, forward(src), src, gain, vector, adj_form),
+        smem=1,
+        remote=1,
+    )
     grad_emission, grad_reflect = call(
         functools.partial(end_kernel, slots, n_x, n_s),
-        [((size, BLK * CONF), F32), ((2, size, PK), F32)],
-        [pltpu.VMEM(blocks(3 * rows), BF16), pltpu.VMEM(blocks(rows), F32), pltpu.VMEM(blocks(size), F32)]
-        + sum_bufs + col_bufs * 2 + [dma((9 + 8 * n_x,))] * 2,
-        (index, part_two, adjoint_one, adj_form, first_sums, view_total, gain),
+        [((size, BLK * CONF), F32), ((size // 2, 128), F32)],
+        bufs + [dma((5 + 4 * n_x,))] * 2,
+        (index, forward(bounced), next_vector, adj_form, first_sums, adjoint_one, view_total),
         smem=1,
         remote=2,
     )
-    return grad_emission, grad_reflect.transpose(1, 2, 0).reshape(size * BLK)
+    return grad_emission, grad_reflect.reshape(size * BLK)
 
 
 def solution(mesh):

time: 119 us -> 96.3 us (0.81)
  Pallas kernels: 109 us -> 87.7 us
  local copies, waits for them, and re-layouts: 7.38 us -> 5.94 us
    pallas_call x5, Pallas kernels: 109 us -> 87.7 us  [call(): pl.pallas_call(kernel, out_shape=[jax.ShapeDtypeStruct(*out) for out in o...]
    broadcast_in_dim x2 -> x4, local copies, waits for them, and re-layouts: 1.49 us -> 0.26 us  [body(): meta = jnp.where(own_list, marks, 0).reshape(n_s, lists * cap)]
    unnamed x11 -> x10, local copies, waits for them, and re-layouts: 4.36 us -> 5.38 us
where the time goes in v2:
time: 96.3 us; the launch traced here: 96.1 us
  Pallas kernels  87.7 us (91%)
  local copies, waits for them, and re-layouts  5.94 us (6%)
  other arithmetic  1.64 us (2%)
    pallas_call x5, Pallas kernels, call(): pl.pallas_call(kernel, out_shape=[jax.ShapeDtypeStruct(*out) for out in o...  87.7 us
    unnamed x10, local copies, waits for them, and re-layouts  5.38 us

profile of v2, /device:TPU:0, one launch (start us, length us, event | category | flops | bytes accessed | tf_op | source)
XLA Modules:
  0.0 96.1 jit_solution(3255846721020759002)
XLA Ops:
  0.7 0.7 broadcast_subtract_fusion
  1.4 0.1 broadcast_in_dim.40
  1.5 0.1 broadcast_in_dim.41
  1.6 0.8 bitcast_select_fusion
  2.3 0.1 sub.50
  2.4 0.1 copy.13
  2.5 0.1 fusion.8
  2.6 0.1 reshape.221.index
  2.7 0.1 broadcast_in_dim.45
  2.8 0.1 fusion
  2.9 0.0 copy-start
  2.9 1.6 %copy-done = bf16[64,1,4,4096]{3,2,1,0:T(4,128)(2,1)S(1)} copy-done((bf16[64,1,4,4096]{3,2,1,0:T(4,128)(2,1)S(1)}, bf16[64,1,4,4096]{3,2,1,0:T(4,128)(2,1)}, u32[]{:S(2)}) %copy-start) | copy-done | bytes 2097176
  4.5 0.0 copy-start.1
  4.5 0.9 copy-done.1
  5.4 0.0 copy-start.2
  5.4 0.9 copy-done.2
  6.3 0.0 copy-start.3
  6.3 0.7 copy-done.3
  7.0 28.3 %shard_map.86 = (bf16[64,32,128]{2,1,0:T(8,128)(2,1)S(1)}, bf16[64,128,128]{2,1,0:T(8,128)(2,1)S(1)}, bf16[64,128,128]{2,1,0:T(8,128)(2,1)S(1)}, f32[16,32,128]{...) custom-call(bf16[16,4096]{1,0:T(8,128)(2,1)S(1)} %copy-done.1, f32[8,128]{1,0:T(8,128)S(1)} %bitcast.21, ...), custom_call_target="tpu_custom_call" | custom-call | tf_op jit(solution)/shard_map/pallas_call | solution.py:504
  35.3 4.0 %shard_map.87.part = bf16[192,32,128]{2,1,0:T(8,128)(2,1)S(1)} custom-call(s32[256]{0:T(256)S(1)} %reshape.221.index, bf16[64,128,128]{2,1,0:T(8,128)(2,1)S(1)} %get-tuple-element.14.form, bf16[64,32,128]{2,1,0:T(8,128)(2,1)S(1)} %get-tuple-element.15.src), custom_call_target="tpu_custom_call" | custom-call | tf_op jit(solution)/shard_map/pallas_call | solution.py:504
  39.3 30.9 %shard_map.88 = (f32[16,32,128]{2,1,0:T(8,128)S(1)}, bf16[64,32,128]{2,1,0:T(8,128)(2,1)S(1)}, f32[16,32,128]{2,1,0:T(8,128)S(1)}, bf16[192,32,128]{2,1,0:T(8,128)(2,1)S(1)}) custom-call(s32[256]{0:T(256)S(1)} %reshape.221.index, bf16[192,32,128]{2,1,0:T(8,128)(2,1)S(1)} %shard_map.87.part, bf16[64,32,128]{2,1,0:T(8,128)(2,1)S(1)} %get-tuple-element.15.src, ...), custom_call_target="tpu_custom_call" | custom-call | tf_op jit(solution)/shard_map/pallas_call | solution.py:504
  70.2 4.0 %shard_map.89.part = bf16[192,32,128]{2,1,0:T(8,128)(2,1)S(1)} custom-call(s32[256]{0:T(256)S(1)} %reshape.221.index, bf16[64,128,128]{2,1,0:T(8,128)(2,1)S(1)} %get-tuple-element.14.form, bf16[64,32,128]{2,1,0:T(8,128)(2,1)S(1)} %get-tuple-element.19.src), custom_call_target="tpu_custom_call" | custom-call | tf_op jit(solution)/shard_map/pallas_call | solution.py:504
  74.2 20.5 %shard_map.90 = (f32[16,4096]{1,0:T(8,128)S(1)}, f32[8,128]{1,0:T(8,128)S(1)}) custom-call(s32[256]{0:T(256)S(1)} %reshape.221.index, bf16[192,32,128]{2,1,0:T(8,128)(2,1)S(1)} %shard_map.89.part, bf16[192,32,128]{2,1,0:T(8,128)(2,1)S(1)} %get-tuple-element.20.vector, bf16[64,128,128]{2,1,0:T(8,128)(2,1)S(1)} %get-tuple-element.18.adj_form, ...), custom_call_target="tpu_custom_call" | custom-call | tf_op jit(solution)/shard_map/pallas_call | solution.py:504
  94.8 0.7 copy.17
  95.5 0.6 copy.18
  (6 shorter events, 0.0 us)
Async XLA Ops:
  2.9 1.6 %copy-start = (bf16[64,1,4,4096]{3,2,1,0:T(4,128)(2,1)S(1)}, bf16[64,1,4,4096]{3,2,1,0:T(4,128)(2,1)}, u32[]{:S(2)}) copy-start(bf16[64,1,4,4096]{3,2,1,0:T(4,128)(2,1)} %param.9) | copy-start | bytes 6291460
  4.5 0.9 copy-start.1
  5.4 0.9 copy-start.2
  6.3 0.7 copy-start.3

commit v3 on v2

--- a/solution.py
+++ b/solution.py
@@ -14,6 +14,7 @@
 F32 = jnp.float32
 BF16 = jnp.bfloat16
 VMEM_BYTES = 32 * 1024 * 1024
+FIRST_BYTES = 44 * 1024 * 1024
 
 
 class Net:
@@ -101,53 +102,68 @@
 
 class GatherWindow:
     def __init__(self, net, buf, n_x, size, n_s):
-        self.net, self.buf, self.n_s = net, buf, n_s
-        self.run = 2 * n_x * size
-        self.group = n_x * size
-        self.col = GatherCol(net, buf, n_x, size, self.run)
-
-    def half(self, run, core):
-        return self.buf.at[pl.ds(run * self.run + core * self.group, self.group)]
-
-    def along(self):
-        s, x, core = place()
-        n_s, net = self.n_s, self.net
-        self.col.arrive_across()
-        self.up = net.copy(self.half(1, core), self.half(0, core), {"space": s + 1})
-        self.down = net.copy(self.half(1, core), self.half(2, core), {"space": s - 1})
-        pl.when(s < n_s - 1)(self.up.start)
-        pl.when(s > 0)(self.down.start)
+        s, x, core = place()
+        self.net, self.buf, self.n_x, self.size, self.n_s = net, buf, n_x, size, n_s
+        self.x, self.core = x, core
+        self.z, self.beside = [], []
+        self.across = []
+        mine = self.piece(1, x)
+        for d in range(1, n_x):
+            cp = net.copy(mine, mine, {"col": 2 * ((x + d) % n_x) + core})
+            cp.start()
+            self.across.append(cp)
+        self.along(x)
+        self.pass_on(mine)
+
+    def piece(self, run, x):
+        start = ((2 * run + self.core) * self.n_x + x) * self.size
+        return self.buf.at[pl.ds(start, self.size)]
+
+    def pass_on(self, piece):
+        cp = self.net.copy(piece, piece, {"col": 2 * self.x + 1 - self.core})
+        cp.start()
+        self.beside.append(cp)
+
+    def along(self, x):
+        s = lax.axis_index("space")
+        up = self.net.copy(self.piece(1, x), self.piece(0, x), {"space": s + 1})
+        down = self.net.copy(self.piece(1, x), self.piece(2, x), {"space": s - 1})
+        pl.when(s < self.n_s - 1)(up.start)
+        pl.when(s > 0)(down.start)
+        self.z.append((up, down, x))
+
+    def arrive_across(self):
+        for d, cp in enumerate(self.across, 1):
+            cp.wait_recv()
+            at = (self.x + self.n_x - d) % self.n_x
+            self.along(at)
+            self.pass_on(self.piece(1, at))
 
     def finish(self):
-        s, x, core = place()
-        n_s, net = self.n_s, self.net
-        other = {"col": 2 * x + 1 - core}
-        before = net.copy(self.half(0, core), self.half(0, core), other)
-        after = net.copy(self.half(2, core), self.half(2, core), other)
-
-        @pl.when(s > 0)
-        def _():
-            self.up.wait_recv()
-            before.start()
-
-        @pl.when(s < n_s - 1)
-        def _():
-            self.down.wait_recv()
-            after.start()
-
-        self.col.finish()
-
-        @pl.when(s > 0)
-        def _():
-            before.wait_recv()
-            before.wait_send()
-            self.down.wait_send()
-
-        @pl.when(s < n_s - 1)
-        def _():
-            after.wait_recv()
-            after.wait_send()
-            self.up.wait_send()
+        s = lax.axis_index("space")
+        below, above = s > 0, s < self.n_s - 1
+        other = {"col": 2 * self.x + 1 - self.core}
+        for up, down, x in self.z:
+            before = self.net.copy(self.piece(0, x), self.piece(0, x), other)
+            after = self.net.copy(self.piece(2, x), self.piece(2, x), other)
+            for there, came, on in ((below, up, before), (above, down, after)):
+
+                @pl.when(there)
+                def _(came=came, on=on):
+                    came.wait_recv()
+                    on.start()
+
+            pl.when(above)(up.wait_send)
+            pl.when(below)(down.wait_send)
+            self.beside.append((below, before))
+            self.beside.append((above, after))
+        for cp in self.beside:
+            if isinstance(cp, tuple):
+                pl.when(cp[0])(cp[1].wait)
+            else:
+                cp.wait()
+        for cp in self.across:
+            cp.wait_send()
 
 
 class SumForward:
@@ -156,79 +172,83 @@
         self.net, self.part, self.got_core = net, part, got_core
         self.z_out, self.z_in, self.x_out, self.x_in = z_out, z_in, x_out, x_in
         self.n_x, self.size, self.n_s = n_x, size, n_s
-        self.run, self.group = 2 * n_x * size, n_x * size
-        group = self.group
-        self.first = []
-        for r in (0, 2, 1):
-            src = part.at[pl.ds(r * self.run + (1 - core) * group, group)]
-            cp = net.copy(src, got_core.at[pl.ds(r * group, group)], {"col": 2 * x + 1 - core})
-            cp.start()
-            self.first.append(cp)
-
-    def pair(self, r, start, count):
-        s, x, core = place()
-        mine = self.part[pl.ds(r * self.run + core * self.group + start, count)]
-        return mine.astype(F32) + self.got_core[pl.ds(r * self.group + start, count)].astype(F32)
+        self.order = [(x + d) % n_x for d in list(range(1, n_x)) + [0]]
+        self.first, self.z = {}, []
+        for d, to in enumerate(self.order):
+            for r in (0, 2, 1):
+                src = part.at[pl.ds(((2 * r + 1 - core) * n_x + to) * size, size)]
+                dst = got_core.at[pl.ds((r * n_x + to) * size, size)]
+                cp = net.copy(src, dst, {"col": 2 * x + 1 - core})
+                cp.start()
+                self.first[d, r] = cp
+
+    def pair(self, r, at):
+        s, x, core = place()
+        n_x, size = self.n_x, self.size
+        mine = self.part[pl.ds(((2 * r + core) * n_x + at) * size, size)]
+        return mine.astype(F32) + self.got_core[pl.ds((r * n_x + at) * size, size)].astype(F32)
 
     def along(self):
         s, x, core = place()
-        group = self.group
-        self.z = [
-            self.net.copy(self.z_out.at[0], self.z_in.at[1], {"space": s - 1}),
-            self.net.copy(self.z_out.at[1], self.z_in.at[0], {"space": s + 1}),
-        ]
-        self.first[0].wait_recv()
-
-        @pl.when(s > 0)
-        def _():
-            self.z_out[0] = self.pair(0, 0, group).astype(BF16)
-            self.z[0].start()
-
-        self.first[1].wait_recv()
-
-        @pl.when(s < self.n_s - 1)
-        def _():
-            self.z_out[1] = self.pair(2, 0, group).astype(BF16)
-            self.z[1].start()
-
-        @pl.when(s == 0)
-        def _():
-            self.z_in[0] = jnp.zeros(self.z_in.shape[1:], BF16)
-
-        @pl.when(s == self.n_s - 1)
-        def _():
-            self.z_in[1] = jnp.zeros(self.z_in.shape[1:], BF16)
-
-    def rows(self, at):
-        start, count = at * self.size, self.size
-        total = self.pair(1, start, count)
+        for side, edge in ((0, s == 0), (1, s == self.n_s - 1)):
+
+            @pl.when(edge)
+            def _(side=side):
+                self.z_in[side] = jnp.zeros(self.z_in.shape[1:], BF16)
+
+        for d, to in enumerate(self.order):
+            rows = pl.ds(to * self.size, self.size)
+            down = self.net.copy(self.z_out.at[0, rows], self.z_in.at[1, rows], {"space": s - 1})
+            up = self.net.copy(self.z_out.at[1, rows], self.z_in.at[0, rows], {"space": s + 1})
+            self.first[d, 0].wait_recv()
+
+            @pl.when(s > 0)
+            def _(down=down, rows=rows, to=to):
+                self.z_out[0, rows] = self.pair(0, to).astype(BF16)
+                down.start()
+
+            self.first[d, 2].wait_recv()
+
+            @pl.when(s < self.n_s - 1)
+            def _(up=up, rows=rows, to=to):
+                self.z_out[1, rows] = self.pair(2, to).astype(BF16)
+                up.start()
+
+            self.z.append((down, up))
+
+    def rows(self, d):
+        s, x, core = place()
+        self.first[d, 1].wait_recv()
+        down, up = self.z[d]
+        pl.when(s > 0)(up.wait_recv)
+        pl.when(s < self.n_s - 1)(down.wait_recv)
+        at = self.order[d]
+        total = self.pair(1, at)
         for side in range(2):
-            total = total + self.z_in[side, pl.ds(start, count)].astype(F32)
+            total = total + self.z_in[side, pl.ds(at * self.size, self.size)].astype(F32)
         return total
 
     def across(self):
         s, x, core = place()
-        self.first[2].wait_recv()
-        pl.when(s > 0)(self.z[1].wait_recv)
-        pl.when(s < self.n_s - 1)(self.z[0].wait_recv)
         self.x = []
-        for d in range(1, self.n_x):
-            to = (x + d) % self.n_x
-            self.x_out[d - 1] = self.rows(to)
-            cp = self.net.copy(self.x_out.at[d - 1], self.x_in.at[d - 1], {"col": 2 * to + core})
+        for d in range(self.n_x - 1):
+            self.x_out[d] = self.rows(d)
+            to = {"col": 2 * self.order[d] + core}
+            cp = self.net.copy(self.x_out.at[d], self.x_in.at[d], to)
             cp.start()
             self.x.append(cp)
 
     def finish(self):
         s, x, core = place()
-        total = self.rows(x)
-        for d in range(1, self.n_x):
-            self.x[d - 1].wait_recv()
-            total = total + self.x_in[d - 1]
-        for cp in self.first + self.x:
+        total = self.rows(self.n_x - 1)
+        for d in range(self.n_x - 1):
+            self.x[d].wait_recv()
+            total = total + self.x_in[d]
+        for cp in list(self.first.values()) + self.x:
             cp.wait_send()
-        pl.when(s > 0)(self.z[0].wait_send)
-        pl.when(s < self.n_s - 1)(self.z[1].wait_send)
+        for down, up in self.z:
+            pl.when(s > 0)(down.wait_send)
+            pl.when(s < self.n_s - 1)(up.wait_send)
         return total
 
 
@@ -284,9 +304,9 @@
 
 
 def start_kernel(
-    n_x, n_s, emission, reflect, view, meta, form, rows_perm, lanes_perm,
+    n_x, n_s, emission_in, view, form_in, reflect, meta, rows_perm, lanes_perm,
     src, fwd_form, adj_form, gain, view_total, vector,
-    views, metas, entries, unpacked, send_sems, recv_sems, local_sem,
+    emission, form, views, metas, entries, unpacked, send_sems, recv_sems, local_sem,
 ):
     s, x, core = place()
     size = emission.shape[0]
@@ -294,15 +314,12 @@
     rows = form.shape[0]
     net = Net(send_sems, recv_sems)
     where = core * n_x + x
-    for i in range(PK):
-        unpacked[:, i, :] = emission[:, i * 128 : (i + 1) * 128].astype(F32)
-    src[pl.ds(where * size, size)] = unpacked[...].astype(BF16)
+    bring = pltpu.make_async_copy(emission_in, emission, local_sem.at[2])
+    bring.start()
+    bring_form = pltpu.make_async_copy(form_in, form, local_sem.at[3])
+    bring_form.start()
+    greet(n_x, True, n_s)
     at = where * n_s + s
-    own_view = pltpu.make_async_copy(view.at[s], views.at[at], local_sem.at[0])
-    own_view.start()
-    own_meta = pltpu.make_async_copy(meta.at[s], metas.at[at], local_sem.at[1])
-    own_meta.start()
-    greet(n_x, True, n_s)
     spread = []
     for d in range(1, n_s):
         to = (s + d) % n_s
@@ -310,6 +327,14 @@
         spread.append(net.copy(meta.at[to], metas.at[at], {"space": to}))
     for cp in spread:
         cp.start()
+    bring.wait()
+    for i in range(PK):
+        unpacked[:, i, :] = emission[:, i * 128 : (i + 1) * 128].astype(F32)
+    src[pl.ds(where * size, size)] = unpacked[...].astype(BF16)
+    own_view = pltpu.make_async_copy(view.at[s], views.at[at], local_sem.at[0])
+    own_view.start()
+    own_meta = pltpu.make_async_copy(meta.at[s], metas.at[at], local_sem.at[1])
+    own_meta.start()
     gather = GatherCol(net, src, n_x, size)
 
     def prepare(j):
@@ -321,6 +346,7 @@
             lanes_perm[...], plain, (((0,), (1,)), ((), ())), preferred_element_type=F32
         ).astype(BF16)
 
+    bring_form.wait()
     loop(0, rows // 4, prepare, 8)
     for p in range(size):
         sel, lanes = patch_masks(p)
@@ -354,7 +380,7 @@
     vector[pl.ds(2 * n_x * size + where * size, size)] = (gain[...] * view_total[...]).astype(BF16)
     window = GatherWindow(net, vector, n_x, size, n_s)
     loop(rows // 2, rows // 4, prepare, 8)
-    window.along()
+    window.arrive_across()
     loop(rows // 2 + rows // 4, rows // 4, prepare, 8)
     window.finish()
     for cp in spread:
@@ -449,7 +475,7 @@
         src[pl.ds(mine, size)].astype(F32) + gain[...] * first_sums[...]
     ).astype(BF16)
     second = GatherCol(net, bounced, n_x, size)
-    gather.along()
+    gather.arrive_across()
     second.arrive_across()
     gather.finish()
     second.finish()
@@ -492,14 +518,16 @@
         grad_reflect[p // 2 : p // 2 + 1, :] = total
 
 
-def call(kernel, outs, scratch, operands, smem=0, remote=None):
+def call(kernel, outs, scratch, operands, smem=0, hbm=0, remote=None, vmem_bytes=VMEM_BYTES):
     vmem = pl.BlockSpec(memory_space=pltpu.VMEM)
-    specs = [pl.BlockSpec(memory_space=pltpu.SMEM)] * smem + [vmem] * (len(operands) - smem)
+    specs = [pl.BlockSpec(memory_space=pltpu.SMEM)] * smem
+    specs += [pl.BlockSpec(memory_space=pltpu.HBM)] * hbm
+    specs += [vmem] * (len(operands) - smem - hbm)
     if remote is None:
-        params = pltpu.CompilerParams(vmem_limit_bytes=VMEM_BYTES)
+        params = pltpu.CompilerParams(vmem_limit_bytes=vmem_bytes)
     else:
         params = pltpu.CompilerParams(
-            vmem_limit_bytes=VMEM_BYTES, collective_id=remote, has_side_effects=True
+            vmem_limit_bytes=vmem_bytes, collective_id=remote, has_side_effects=True
         )
     return pl.pallas_call(
         kernel,
@@ -550,13 +578,17 @@
             (blocks(3 * rows), BF16),
         ],
         [
+            pltpu.VMEM(emission.shape, BF16),
+            pltpu.VMEM(form.shape, BF16),
             pltpu.VMEM((lists, cap, BLK * CONF), BF16),
             pltpu.VMEM((lists,) + meta.shape[1:], jnp.int32),
             pltpu.VMEM((lists * cap, BLK * CONF), F32),
             pltpu.VMEM(blocks(size), F32),
         ]
-        + [dma((4 + 2 * n_s + 8 * n_x,))] * 2 + [dma((2,))],
-        (emission, reflect.reshape(-1, 128), view_grads[0, 0], meta, form, rows_perm, lanes_perm),
+        + [dma((2 * n_s + 12 * n_x,))] * 2 + [dma((4,))],
+        (emission, view_grads[0, 0], form, reflect.reshape(-1, 128), meta, rows_perm, lanes_perm),
+        hbm=3,
+        vmem_bytes=FIRST_BYTES,
         remote=0,
     )
     group = n_x * size
@@ -589,7 +621,7 @@
             (blocks(size), F32),
             (blocks(3 * rows), BF16),
         ],
-        bufs + [dma((9 + 8 * n_x,))] * 2,
+        bufs + [dma((16 * n_x,))] * 2,
         (index, forward(src), src, gain, vector, adj_form),
         smem=1,
         remote=1,
@@ -597,7 +629,7 @@
     grad_emission, grad_reflect = call(
         functools.partial(end_kernel, slots, n_x, n_s),
         [((size, BLK * CONF), F32), ((size // 2, 128), F32)],
-        bufs + [dma((5 + 4 * n_x,))] * 2,
+        bufs + [dma((8 * n_x,))] * 2,
         (index, forward(bounced), next_vector, adj_form, first_sums, adjoint_one, view_total),
         smem=1,
         remote=2,

time: 96.3 us -> 90.8 us (0.943)
  Pallas kernels: 87.7 us -> 82.2 us
    pallas_call x5, Pallas kernels: 87.7 us -> 82.2 us  [call(): pl.pallas_call(kernel, out_shape=[jax.ShapeDtypeStruct(*out) for out in o...]
where the time goes in v3:
time: 90.8 us; the launch traced here: 90.6 us
  Pallas kernels  82.2 us (91%)
  local copies, waits for them, and re-layouts  5.94 us (7%)
  other arithmetic  1.64 us (2%)
    pallas_call x5, Pallas kernels, call(): pl.pallas_call(kernel, out_shape=[jax.ShapeDtypeStruct(*out) for out in o...  82.2 us
    unnamed x10, local copies, waits for them, and re-layouts  5.38 us

profile of v3, /device:TPU:0, one launch (start us, length us, event | category | flops | bytes accessed | tf_op | source)
XLA Modules:
  0.0 90.6 jit_solution(1050605025450023945)
XLA Ops:
  0.7 0.7 broadcast_subtract_fusion
  1.4 0.1 broadcast_in_dim.40
  1.5 0.1 broadcast_in_dim.41
  1.6 0.8 bitcast_select_fusion
  2.3 0.1 sub.50
  2.4 0.1 copy.13
  2.5 0.1 fusion.8
  2.6 0.1 reshape.221.index
  2.7 0.1 broadcast_in_dim.45
  2.8 0.1 fusion
  2.9 0.0 copy-start
  2.9 1.6 %copy-done = bf16[64,1,4,4096]{3,2,1,0:T(4,128)(2,1)S(1)} copy-done((bf16[64,1,4,4096]{3,2,1,0:T(4,128)(2,1)S(1)}, bf16[64,1,4,4096]{3,2,1,0:T(4,128)(2,1)}, u32[]{:S(2)}) %copy-start) | copy-done | bytes 2097176
  4.5 0.0 copy-start.1
  4.5 0.9 copy-done.1
  5.4 0.0 copy-start.2
  5.4 0.9 copy-done.2
  6.3 0.0 copy-start.3
  6.3 0.7 copy-done.3
  7.0 25.4 %shard_map.86 = (bf16[64,32,128]{2,1,0:T(8,128)(2,1)S(1)}, bf16[64,128,128]{2,1,0:T(8,128)(2,1)S(1)}, bf16[64,128,128]{2,1,0:T(8,128)(2,1)S(1)}, f32[16,32,128]{...) custom-call(bf16[16,4096]{1,0:T(8,128)(2,1)S(1)} %copy-done.1, ...), custom_call_target="tpu_custom_call" | custom-call | tf_op jit(solution)/shard_map/pallas_call | solution.py:532
  32.4 4.0 %shard_map.87.part = bf16[192,32,128]{2,1,0:T(8,128)(2,1)S(1)} custom-call(s32[256]{0:T(256)S(1)} %reshape.221.index, bf16[64,128,128]{2,1,0:T(8,128)(2,1)S(1)} %get-tuple-element.14.form, bf16[64,32,128]{2,1,0:T(8,128)(2,1)S(1)} %get-tuple-element.15.src), custom_call_target="tpu_custom_call" | custom-call | tf_op jit(solution)/shard_map/pallas_call | solution.py:532
  36.4 28.6 %shard_map.88 = (f32[16,32,128]{2,1,0:T(8,128)S(1)}, bf16[64,32,128]{2,1,0:T(8,128)(2,1)S(1)}, f32[16,32,128]{2,1,0:T(8,128)S(1)}, bf16[192,32,128]{2,1,0:T(8,128)(2,1)S(1)}) custom-call(s32[256]{0:T(256)S(1)} %reshape.221.index, bf16[192,32,128]{2,1,0:T(8,128)(2,1)S(1)} %shard_map.87.part, bf16[64,32,128]{2,1,0:T(8,128)(2,1)S(1)} %get-tuple-element.15.src, ...), custom_call_target="tpu_custom_call" | custom-call | tf_op jit(solution)/shard_map/pallas_call | solution.py:532
  65.1 4.0 %shard_map.89.part = bf16[192,32,128]{2,1,0:T(8,128)(2,1)S(1)} custom-call(s32[256]{0:T(256)S(1)} %reshape.221.index, bf16[64,128,128]{2,1,0:T(8,128)(2,1)S(1)} %get-tuple-element.14.form, bf16[64,32,128]{2,1,0:T(8,128)(2,1)S(1)} %get-tuple-element.19.src), custom_call_target="tpu_custom_call" | custom-call | tf_op jit(solution)/shard_map/pallas_call | solution.py:532
  69.1 20.2 %shard_map.90 = (f32[16,4096]{1,0:T(8,128)S(1)}, f32[8,128]{1,0:T(8,128)S(1)}) custom-call(s32[256]{0:T(256)S(1)} %reshape.221.index, bf16[192,32,128]{2,1,0:T(8,128)(2,1)S(1)} %shard_map.89.part, bf16[192,32,128]{2,1,0:T(8,128)(2,1)S(1)} %get-tuple-element.20.vector, bf16[64,128,128]{2,1,0:T(8,128)(2,1)S(1)} %get-tuple-element.18.adj_form, ...), custom_call_target="tpu_custom_call" | custom-call | tf_op jit(solution)/shard_map/pallas_call | solution.py:532
  89.3 0.7 copy.17
  90.0 0.6 copy.18
  (6 shorter events, 0.0 us)
Async XLA Ops:
  2.9 1.6 %copy-start = (bf16[64,1,4,4096]{3,2,1,0:T(4,128)(2,1)S(1)}, bf16[64,1,4,4096]{3,2,1,0:T(4,128)(2,1)}, u32[]{:S(2)}) copy-start(bf16[64,1,4,4096]{3,2,1,0:T(4,128)(2,1)} %param.9) | copy-start | bytes 6291460
  4.5 0.9 copy-start.1
  5.4 0.9 copy-start.2
  6.3 0.7 copy-start.3

commit v4 on v3

--- a/solution.py
+++ b/solution.py
@@ -14,7 +14,7 @@
 F32 = jnp.float32
 BF16 = jnp.bfloat16
 VMEM_BYTES = 32 * 1024 * 1024
-FIRST_BYTES = 44 * 1024 * 1024
+FIRST_BYTES = 48 * 1024 * 1024
 
 
 class Net:
@@ -337,30 +337,40 @@
     own_meta.start()
     gather = GatherCol(net, src, n_x, size)
 
-    def prepare(j):
+    def prepare(t):
+        j = t * 8
         c, r = j // size, j % size
         to = ((c % 2) * n_x + c // 2) * size + r
-        plain = jnp.dot(rows_perm[...], form[j], preferred_element_type=F32).astype(BF16)
-        fwd_form[to] = jnp.dot(plain, lanes_perm[...], preferred_element_type=F32).astype(BF16)
-        adj_form[to] = lax.dot_general(
-            lanes_perm[...], plain, (((0,), (1,)), ((), ())), preferred_element_type=F32
-        ).astype(BF16)
-
+        plain = [
+            jnp.dot(rows_perm[...], form[j + u], preferred_element_type=F32).astype(BF16)
+            for u in range(8)
+        ]
+        tall = jnp.concatenate(plain, axis=0)
+        turned = jnp.dot(tall, lanes_perm[...], preferred_element_type=F32).astype(BF16)
+        for u in range(8):
+            fwd_form[to + u] = turned[u * tall.shape[0] // 8 : (u + 1) * tall.shape[0] // 8]
+            adj_form[to + u] = lax.dot_general(
+                lanes_perm[...], plain[u], (((0,), (1,)), ((), ())), preferred_element_type=F32
+            ).astype(BF16)
+
+    eighth = rows // 8
     bring_form.wait()
-    loop(0, rows // 4, prepare, 8)
-    for p in range(size):
-        sel, lanes = patch_masks(p)
-        picked = jnp.where(sel, reflect[p // 2 : p // 2 + 1, :], 0.0)
-        gain[p] = jnp.dot(
-            picked, lanes, preferred_element_type=F32, precision=lax.Precision.HIGHEST
-        )
+    loop(0, eighth // 4, prepare, 1)
     own_view.wait()
     own_meta.wait()
     for cp in spread:
         cp.wait_recv()
     more = [GatherCol(net, views, n_x, n_s), GatherCol(net, metas, n_x, n_s)]
     gather.arrive_across()
-    loop(rows // 4, rows // 4, prepare, 8)
+    picked = []
+    for p in range(size):
+        sel, lanes = patch_masks(p)
+        picked.append(jnp.where(sel, reflect[p // 2 : p // 2 + 1, :], 0.0))
+    gain[...] = jnp.dot(
+        jnp.concatenate(picked, axis=0), lanes,
+        preferred_element_type=F32, precision=lax.Precision.HIGHEST,
+    ).reshape(gain.shape)
+    loop(eighth // 4, eighth // 4, prepare, 1)
     for g in more:
         g.arrive_across()
     gather.finish()
@@ -379,9 +389,9 @@
             view_total[:, i + u, :] = found[:, u * 128 : (u + 1) * 128]
     vector[pl.ds(2 * n_x * size + where * size, size)] = (gain[...] * view_total[...]).astype(BF16)
     window = GatherWindow(net, vector, n_x, size, n_s)
-    loop(rows // 2, rows // 4, prepare, 8)
+    loop(eighth // 2, eighth // 4, prepare, 1)
     window.arrive_across()
-    loop(rows // 2 + rows // 4, rows // 4, prepare, 8)
+    loop(eighth // 2 + eighth // 4, eighth // 4, prepare, 1)
     window.finish()
     for cp in spread:
         cp.wait_send()
@@ -505,16 +515,18 @@
     keep[pl.ds(0, size)] = view_total[...] + adjoint_one[...] + got_two
     for i in range(PK):
         grad_emission[:, i * 128 : (i + 1) * 128] = keep[:size, i, :]
-    keep[pl.ds(0, size)] = view_total[...] * sums.finish() + adjoint_one[...] * first_sums[...]
+    product = view_total[...] * sums.finish() + adjoint_one[...] * first_sums[...]
+    lanes = patch_masks(0)[1]
+    halves = lax.dot_general(
+        product.reshape(size * PK, 128), lanes, (((1,), (1,)), ((), ())),
+        preferred_element_type=F32, precision=lax.Precision.HIGHEST,
+    )
     for p in range(0, size, 2):
         total = jnp.zeros((1, 128), F32)
         for q in (p, p + 1):
-            sel, lanes = patch_masks(q)
-            spread = lax.dot_general(
-                keep[q], lanes, (((1,), (1,)), ((), ())),
-                preferred_element_type=F32, precision=lax.Precision.HIGHEST,
-            )
-            total = total + jnp.sum(jnp.where(sel, spread, 0.0), axis=0, keepdims=True)
+            sel = patch_masks(q)[0]
+            part_q = jnp.where(sel, halves[q * PK : (q + 1) * PK], 0.0)
+            total = total + jnp.sum(part_q, axis=0, keepdims=True)
         grad_reflect[p // 2 : p // 2 + 1, :] = total
 
 

time: 90.8 us -> 89.1 us (0.981)
  local copies, waits for them, and re-layouts: 5.94 us -> 4.35 us
    unnamed x10, local copies, waits for them, and re-layouts: 5.38 us -> 3.79 us
where the time goes in v4:
time: 89.1 us; the launch traced here: 88.9 us
  Pallas kernels  82.1 us (92%)
  local copies, waits for them, and re-layouts  4.35 us (5%)
  other arithmetic  1.64 us (2%)
    pallas_call x5, Pallas kernels, call(): pl.pallas_call(kernel, out_shape=[jax.ShapeDtypeStruct(*out) for out in o...  82.1 us
    unnamed x10, local copies, waits for them, and re-layouts  3.79 us

profile of v4, /device:TPU:0, one launch (start us, length us, event | category | flops | bytes accessed | tf_op | source)
XLA Modules:
  0.0 88.9 jit_solution(6893713154092465272)
XLA Ops:
  0.7 0.7 broadcast_subtract_fusion
  1.4 0.1 broadcast_in_dim.40
  1.5 0.1 broadcast_in_dim.41
  1.6 0.8 bitcast_select_fusion
  2.3 0.1 sub.50
  2.4 0.1 copy.13
  2.5 0.1 fusion.8
  2.6 0.1 reshape.221.index
  2.7 0.1 broadcast_in_dim.45
  2.8 0.1 fusion
  2.9 0.0 copy-start.1
  2.9 0.9 %copy-done.1 = bf16[16,4096]{1,0:T(8,128)(2,1)S(1)} copy-done((bf16[16,4096]{1,0:T(8,128)(2,1)S(1)}, bf16[16,4096]{1,0:T(8,128)(2,1)}, u32[]{:S(2)}) %copy-start.1) | copy-done | bytes 131096
  3.8 0.0 copy-start.2
  3.8 0.9 %copy-done.2 = bf16[1,1,4,4,4096]{4,3,2,1,0:T(4,128)(2,1)S(1)} copy-done((bf16[1,1,4,4,4096]{4,3,2,1,0:T(4,128)(2,1)S(1)}, bf16[1,1,4,4,4096]{4,3,2,1,0:T(4,128)(2,1)}, u32[]{:S(2)}) %copy-start.2) | copy-done | bytes 131096
  4.7 0.0 copy-start.3
  4.7 0.7 copy-done.3
  5.4 26.6 %shard_map.86 = (bf16[64,32,128]{2,1,0:T(8,128)(2,1)S(1)}, bf16[64,128,128]{2,1,0:T(8,128)(2,1)S(1)}, bf16[64,128,128]{2,1,0:T(8,128)(2,1)}, f32[16,32,128]{2,1,...) custom-call(bf16[16,4096]{1,0:T(8,128)(2,1)S(1)} %copy-done.1, ...), custom_call_target="tpu_custom_call" | custom-call | tf_op jit(solution)/shard_map/pallas_call | solution.py:544
  32.0 0.0 copy-start
  32.1 4.0 %shard_map.87.part = bf16[192,32,128]{2,1,0:T(8,128)(2,1)S(1)} custom-call(s32[256]{0:T(256)S(1)} %reshape.221.index, bf16[64,128,128]{2,1,0:T(8,128)(2,1)S(1)} %get-tuple-element.14.form, bf16[64,32,128]{2,1,0:T(8,128)(2,1)S(1)} %get-tuple-element.15.src), custom_call_target="tpu_custom_call" | custom-call | tf_op jit(solution)/shard_map/pallas_call | solution.py:544
  36.1 0.0 copy-done
  36.1 28.6 %shard_map.88 = (f32[16,32,128]{2,1,0:T(8,128)S(1)}, bf16[64,32,128]{2,1,0:T(8,128)(2,1)S(1)}, f32[16,32,128]{2,1,0:T(8,128)S(1)}, bf16[192,32,128]{2,1,0:T(8,128)(2,1)S(1)}) custom-call(s32[256]{0:T(256)S(1)} %reshape.221.index, bf16[192,32,128]{2,1,0:T(8,128)(2,1)S(1)} %shard_map.87.part, bf16[64,32,128]{2,1,0:T(8,128)(2,1)S(1)} %get-tuple-element.15.src, ...), custom_call_target="tpu_custom_call" | custom-call | tf_op jit(solution)/shard_map/pallas_call | solution.py:544
  64.7 4.0 %shard_map.89.part = bf16[192,32,128]{2,1,0:T(8,128)(2,1)S(1)} custom-call(s32[256]{0:T(256)S(1)} %reshape.221.index, bf16[64,128,128]{2,1,0:T(8,128)(2,1)S(1)} %get-tuple-element.14.form, bf16[64,32,128]{2,1,0:T(8,128)(2,1)S(1)} %get-tuple-element.19.src), custom_call_target="tpu_custom_call" | custom-call | tf_op jit(solution)/shard_map/pallas_call | solution.py:544
  68.7 18.9 %shard_map.90 = (f32[16,4096]{1,0:T(8,128)S(1)}, f32[8,128]{1,0:T(8,128)S(1)}) custom-call(s32[256]{0:T(256)S(1)} %reshape.221.index, bf16[192,32,128]{2,1,0:T(8,128)(2,1)S(1)} %shard_map.89.part, bf16[192,32,128]{2,1,0:T(8,128)(2,1)S(1)} %get-tuple-element.20.vector, bf16[64,128,128]{2,1,0:T(8,128)(2,1)S(1)} %copy-done, ...), custom_call_target="tpu_custom_call" | custom-call | tf_op jit(solution)/shard_map/pallas_call | solution.py:544
  87.6 0.7 copy.17
  88.3 0.6 copy.18
  (6 shorter events, 0.0 us)
Async XLA Ops:
  2.9 0.9 %copy-start.1 = (bf16[16,4096]{1,0:T(8,128)(2,1)S(1)}, bf16[16,4096]{1,0:T(8,128)(2,1)}, u32[]{:S(2)}) copy-start(bf16[16,4096]{1,0:T(8,128)(2,1)} %emission_in.1) | copy-start | bytes 393220
  3.8 0.9 %copy-start.2 = (bf16[1,1,4,4,4096]{4,3,2,1,0:T(4,128)(2,1)S(1)}, bf16[1,1,4,4,4096]{4,3,2,1,0:T(4,128)(2,1)}, u32[]{:S(2)}) copy-start(bf16[1,1,4,4,4096]{4,3,2,1,0:T(4,128)(2,1)} %param.11) | copy-start | bytes 393220
  4.7 0.7 copy-start.3
  32.0 4.0 %copy-start = (bf16[64,128,128]{2,1,0:T(8,128)(2,1)S(1)}, bf16[64,128,128]{2,1,0:T(8,128)(2,1)}, u32[]{:S(2)}) copy-start(bf16[64,128,128]{2,1,0:T(8,128)(2,1)} %get-tuple-element.18.adj_form) | copy-start | bytes 6291460

commit v5 on v4

--- a/solution.py
+++ b/solution.py
@@ -258,13 +258,16 @@
         self.net, self.part, self.got_core = net, part, got_core
         self.x_out, self.x_in, self.n_x, self.size = x_out, x_in, n_x, size
         self.group = n_x * size
-        self.first = []
-        for d in list(range(1, n_x)) + [0]:
-            to = (x + d) % n_x
-            src = part.at[pl.ds((1 - core) * self.group + to * size, size)]
-            cp = net.copy(src, got_core.at[pl.ds(to * size, size)], {"col": 2 * x + 1 - core})
-            cp.start()
-            self.first.append(cp)
+        self.net = net
+        self.first, self.x = [], []
+
+    def beside(self, to):
+        s, x, core = place()
+        src = self.part.at[pl.ds((1 - core) * self.group + to * self.size, self.size)]
+        dst = self.got_core.at[pl.ds(to * self.size, self.size)]
+        cp = self.net.copy(src, dst, {"col": 2 * x + 1 - core})
+        cp.start()
+        self.first.append(cp)
 
     def rows(self, at):
         s, x, core = place()
@@ -273,7 +276,6 @@
 
     def across(self):
         s, x, core = place()
-        self.x = []
         for d in range(1, self.n_x):
             to = (x + d) % self.n_x
             self.first[d - 1].wait_recv()
@@ -457,6 +459,21 @@
     write_part(window, part)
 
 
+def adjoint_beside(col_sum, sums, step, n_x, size):
+    s, x, core = place()
+    others = [(x + d) % n_x for d in range(1, n_x)]
+    for to in others:
+        loop(((1 - core) * n_x + to) * size, size, step, 8)
+        col_sum.beside(to)
+    sums.along()
+    for to in others:
+        loop((core * n_x + to) * size, size, step, 8)
+    col_sum.across()
+    loop(((1 - core) * n_x + x) * size, size, step, 8)
+    col_sum.beside(x)
+    loop((core * n_x + x) * size, size, step, 8)
+
+
 def middle_kernel(
     slots, n_x, n_s, index, part, src, gain, vector, adj_form,
     first_sums, bounced, adjoint_one, next_vector,
@@ -471,11 +488,8 @@
     group = n_x * size
     step = lambda j: adjoint_step(j, adj_form, vector, index, slots, terms)
     sums = SumForward(net, part, got_core, z_out, z_in, x_out, x_in, n_x, size, n_s)
-    loop((1 - core) * group, group, step, 8)
     one = SumCol(net, terms, one_core, one_out, one_in, n_x, size)
-    sums.along()
-    loop(core * group, group, step, 8)
-    one.across()
+    adjoint_beside(one, sums, step, n_x, size)
     sums.across()
     adjoint_one[...] = one.finish()
     next_vector[pl.ds(2 * group + mine, size)] = (gain[...] * adjoint_one[...]).astype(BF16)
@@ -504,11 +518,8 @@
     group = n_x * size
     step = lambda j: adjoint_step(j, adj_form, vector, index, slots, terms)
     sums = SumForward(net, part, got_core, z_out, z_in, x_out, x_in, n_x, size, n_s)
-    loop((1 - core) * group, group, step, 8)
     two = SumCol(net, terms, two_core, two_out, two_in, n_x, size)
-    sums.along()
-    loop(core * group, group, step, 8)
-    two.across()
+    adjoint_beside(two, sums, step, n_x, size)
     sums.across()
     got_two = two.finish()
     keep = two_core

time: 89.1 us -> 87.9 us (0.987)
  Pallas kernels: 82.1 us -> 80.9 us
    pallas_call x5, Pallas kernels: 82.1 us -> 80.9 us  [call(): pl.pallas_call(kernel, out_shape=[jax.ShapeDtypeStruct(*out) for out in o...]
where the time goes in v5:
time: 87.9 us; the launch traced here: 87.6 us
  Pallas kernels  80.9 us (92%)
  local copies, waits for them, and re-layouts  4.35 us (5%)
  other arithmetic  1.64 us (2%)
    pallas_call x5, Pallas kernels, call(): pl.pallas_call(kernel, out_shape=[jax.ShapeDtypeStruct(*out) for out in o...  80.9 us
    unnamed x10, local copies, waits for them, and re-layouts  3.79 us

profile of v5, /device:TPU:0, one launch (start us, length us, event | category | flops | bytes accessed | tf_op | source)
XLA Modules:
  0.0 87.6 jit_solution(17752263202702030297)
XLA Ops:
  0.7 0.7 broadcast_subtract_fusion
  1.4 0.1 broadcast_in_dim.40
  1.5 0.1 broadcast_in_dim.41
  1.6 0.8 bitcast_select_fusion
  2.3 0.1 sub.50
  2.4 0.1 copy.13
  2.5 0.1 fusion.8
  2.6 0.1 reshape.221.index
  2.7 0.1 broadcast_in_dim.45
  2.8 0.1 fusion
  2.9 0.0 copy-start.1
  2.9 0.9 %copy-done.1 = bf16[16,4096]{1,0:T(8,128)(2,1)S(1)} copy-done((bf16[16,4096]{1,0:T(8,128)(2,1)S(1)}, bf16[16,4096]{1,0:T(8,128)(2,1)}, u32[]{:S(2)}) %copy-start.1) | copy-done | bytes 131096
  3.8 0.0 copy-start.2
  3.8 0.9 %copy-done.2 = bf16[1,1,4,4,4096]{4,3,2,1,0:T(4,128)(2,1)S(1)} copy-done((bf16[1,1,4,4,4096]{4,3,2,1,0:T(4,128)(2,1)S(1)}, bf16[1,1,4,4,4096]{4,3,2,1,0:T(4,128)(2,1)}, u32[]{:S(2)}) %copy-start.2) | copy-done | bytes 131096
  4.7 0.0 copy-start.3
  4.7 0.7 copy-done.3
  5.4 26.6 %shard_map.86 = (bf16[64,32,128]{2,1,0:T(8,128)(2,1)S(1)}, bf16[64,128,128]{2,1,0:T(8,128)(2,1)S(1)}, bf16[64,128,128]{2,1,0:T(8,128)(2,1)}, f32[16,32,128]{2,1,...) custom-call(bf16[16,4096]{1,0:T(8,128)(2,1)S(1)} %copy-done.1, ...), custom_call_target="tpu_custom_call" | custom-call | tf_op jit(solution)/shard_map/pallas_call | solution.py:555
  32.0 0.0 copy-start
  32.1 4.0 %shard_map.87.part = bf16[192,32,128]{2,1,0:T(8,128)(2,1)S(1)} custom-call(s32[256]{0:T(256)S(1)} %reshape.221.index, bf16[64,128,128]{2,1,0:T(8,128)(2,1)S(1)} %get-tuple-element.14.form, bf16[64,32,128]{2,1,0:T(8,128)(2,1)S(1)} %get-tuple-element.15.src), custom_call_target="tpu_custom_call" | custom-call | tf_op jit(solution)/shard_map/pallas_call | solution.py:555
  36.1 0.0 copy-done
  36.1 28.0 %shard_map.88 = (f32[16,32,128]{2,1,0:T(8,128)S(1)}, bf16[64,32,128]{2,1,0:T(8,128)(2,1)S(1)}, f32[16,32,128]{2,1,0:T(8,128)S(1)}, bf16[192,32,128]{2,1,0:T(8,128)(2,1)S(1)}) custom-call(s32[256]{0:T(256)S(1)} %reshape.221.index, bf16[192,32,128]{2,1,0:T(8,128)(2,1)S(1)} %shard_map.87.part, bf16[64,32,128]{2,1,0:T(8,128)(2,1)S(1)} %get-tuple-element.15.src, ...), custom_call_target="tpu_custom_call" | custom-call | tf_op jit(solution)/shard_map/pallas_call | solution.py:555
  64.1 4.0 %shard_map.89.part = bf16[192,32,128]{2,1,0:T(8,128)(2,1)S(1)} custom-call(s32[256]{0:T(256)S(1)} %reshape.221.index, bf16[64,128,128]{2,1,0:T(8,128)(2,1)S(1)} %get-tuple-element.14.form, bf16[64,32,128]{2,1,0:T(8,128)(2,1)S(1)} %get-tuple-element.19.src), custom_call_target="tpu_custom_call" | custom-call | tf_op jit(solution)/shard_map/pallas_call | solution.py:555
  68.1 18.2 %shard_map.90 = (f32[16,4096]{1,0:T(8,128)S(1)}, f32[8,128]{1,0:T(8,128)S(1)}) custom-call(s32[256]{0:T(256)S(1)} %reshape.221.index, bf16[192,32,128]{2,1,0:T(8,128)(2,1)S(1)} %shard_map.89.part, bf16[192,32,128]{2,1,0:T(8,128)(2,1)S(1)} %get-tuple-element.20.vector, bf16[64,128,128]{2,1,0:T(8,128)(2,1)S(1)} %copy-done, ...), custom_call_target="tpu_custom_call" | custom-call | tf_op jit(solution)/shard_map/pallas_call | solution.py:555
  86.3 0.7 copy.17
  87.0 0.6 copy.18
  (6 shorter events, 0.0 us)
Async XLA Ops:
  2.9 0.9 %copy-start.1 = (bf16[16,4096]{1,0:T(8,128)(2,1)S(1)}, bf16[16,4096]{1,0:T(8,128)(2,1)}, u32[]{:S(2)}) copy-start(bf16[16,4096]{1,0:T(8,128)(2,1)} %emission_in.1) | copy-start | bytes 393220
  3.8 0.9 %copy-start.2 = (bf16[1,1,4,4,4096]{4,3,2,1,0:T(4,128)(2,1)S(1)}, bf16[1,1,4,4,4096]{4,3,2,1,0:T(4,128)(2,1)}, u32[]{:S(2)}) copy-start(bf16[1,1,4,4,4096]{4,3,2,1,0:T(4,128)(2,1)} %param.11) | copy-start | bytes 393220
  4.7 0.7 copy-start.3
  32.0 4.0 %copy-start = (bf16[64,128,128]{2,1,0:T(8,128)(2,1)S(1)}, bf16[64,128,128]{2,1,0:T(8,128)(2,1)}, u32[]{:S(2)}) copy-start(bf16[64,128,128]{2,1,0:T(8,128)(2,1)} %get-tuple-element.18.adj_form) | copy-start | bytes 6291460

commit v6 on v5

--- a/solution.py
+++ b/solution.py
@@ -375,7 +375,6 @@
     loop(eighth // 4, eighth // 4, prepare, 1)
     for g in more:
         g.arrive_across()
-    gather.finish()
     for g in more:
         g.finish()
     count = views.shape[0] * cap
@@ -395,6 +394,7 @@
     window.arrive_across()
     loop(eighth // 2 + eighth // 4, eighth // 4, prepare, 1)
     window.finish()
+    gather.finish()
     for cp in spread:
         cp.wait_send()
 

time: 87.9 us -> 87.9 us (level)
  no operation moved by 1% of the time
where the time goes in v6:
time: 87.9 us; the launch traced here: 87.6 us
  Pallas kernels  80.9 us (92%)
  local copies, waits for them, and re-layouts  4.35 us (5%)
  other arithmetic  1.64 us (2%)
    pallas_call x5, Pallas kernels, call(): pl.pallas_call(kernel, out_shape=[jax.ShapeDtypeStruct(*out) for out in o...  80.9 us
    unnamed x10, local copies, waits for them, and re-layouts  3.79 us

profile of v6, /device:TPU:0, one launch (start us, length us, event | category | flops | bytes accessed | tf_op | source)
XLA Modules:
  0.0 87.6 jit_solution(9906543993407160961)
XLA Ops:
  0.7 0.7 broadcast_subtract_fusion
  1.4 0.1 broadcast_in_dim.40
  1.5 0.1 broadcast_in_dim.41
  1.6 0.8 bitcast_select_fusion
  2.3 0.1 sub.50
  2.4 0.1 copy.13
  2.5 0.1 fusion.8
  2.6 0.1 reshape.221.index
  2.7 0.1 broadcast_in_dim.45
  2.8 0.1 fusion
  2.9 0.0 copy-start.1
  2.9 0.9 %copy-done.1 = bf16[16,4096]{1,0:T(8,128)(2,1)S(1)} copy-done((bf16[16,4096]{1,0:T(8,128)(2,1)S(1)}, bf16[16,4096]{1,0:T(8,128)(2,1)}, u32[]{:S(2)}) %copy-start.1) | copy-done | bytes 131096
  3.8 0.0 copy-start.2
  3.8 0.9 %copy-done.2 = bf16[1,1,4,4,4096]{4,3,2,1,0:T(4,128)(2,1)S(1)} copy-done((bf16[1,1,4,4,4096]{4,3,2,1,0:T(4,128)(2,1)S(1)}, bf16[1,1,4,4,4096]{4,3,2,1,0:T(4,128)(2,1)}, u32[]{:S(2)}) %copy-start.2) | copy-done | bytes 131096
  4.7 0.0 copy-start.3
  4.7 0.7 copy-done.3
  5.4 26.6 %shard_map.86 = (bf16[64,32,128]{2,1,0:T(8,128)(2,1)S(1)}, bf16[64,128,128]{2,1,0:T(8,128)(2,1)S(1)}, bf16[64,128,128]{2,1,0:T(8,128)(2,1)}, f32[16,32,128]{2,1,...) custom-call(bf16[16,4096]{1,0:T(8,128)(2,1)S(1)} %copy-done.1, ...), custom_call_target="tpu_custom_call" | custom-call | tf_op jit(solution)/shard_map/pallas_call | solution.py:555
  32.1 0.0 copy-start
  32.1 4.0 %shard_map.87.part = bf16[192,32,128]{2,1,0:T(8,128)(2,1)S(1)} custom-call(s32[256]{0:T(256)S(1)} %reshape.221.index, bf16[64,128,128]{2,1,0:T(8,128)(2,1)S(1)} %get-tuple-element.14.form, bf16[64,32,128]{2,1,0:T(8,128)(2,1)S(1)} %get-tuple-element.15.src), custom_call_target="tpu_custom_call" | custom-call | tf_op jit(solution)/shard_map/pallas_call | solution.py:555
  36.1 0.0 copy-done
  36.1 28.0 %shard_map.88 = (f32[16,32,128]{2,1,0:T(8,128)S(1)}, bf16[64,32,128]{2,1,0:T(8,128)(2,1)S(1)}, f32[16,32,128]{2,1,0:T(8,128)S(1)}, bf16[192,32,128]{2,1,0:T(8,128)(2,1)S(1)}) custom-call(s32[256]{0:T(256)S(1)} %reshape.221.index, bf16[192,32,128]{2,1,0:T(8,128)(2,1)S(1)} %shard_map.87.part, bf16[64,32,128]{2,1,0:T(8,128)(2,1)S(1)} %get-tuple-element.15.src, ...), custom_call_target="tpu_custom_call" | custom-call | tf_op jit(solution)/shard_map/pallas_call | solution.py:555
  64.1 4.0 %shard_map.89.part = bf16[192,32,128]{2,1,0:T(8,128)(2,1)S(1)} custom-call(s32[256]{0:T(256)S(1)} %reshape.221.index, bf16[64,128,128]{2,1,0:T(8,128)(2,1)S(1)} %get-tuple-element.14.form, bf16[64,32,128]{2,1,0:T(8,128)(2,1)S(1)} %get-tuple-element.19.src), custom_call_target="tpu_custom_call" | custom-call | tf_op jit(solution)/shard_map/pallas_call | solution.py:555
  68.1 18.2 %shard_map.90 = (f32[16,4096]{1,0:T(8,128)S(1)}, f32[8,128]{1,0:T(8,128)S(1)}) custom-call(s32[256]{0:T(256)S(1)} %reshape.221.index, bf16[192,32,128]{2,1,0:T(8,128)(2,1)S(1)} %shard_map.89.part, bf16[192,32,128]{2,1,0:T(8,128)(2,1)S(1)} %get-tuple-element.20.vector, bf16[64,128,128]{2,1,0:T(8,128)(2,1)S(1)} %copy-done, ...), custom_call_target="tpu_custom_call" | custom-call | tf_op jit(solution)/shard_map/pallas_call | solution.py:555
  86.3 0.7 copy.17
  87.0 0.6 copy.18
  (6 shorter events, 0.0 us)
Async XLA Ops:
  2.9 0.9 %copy-start.1 = (bf16[16,4096]{1,0:T(8,128)(2,1)S(1)}, bf16[16,4096]{1,0:T(8,128)(2,1)}, u32[]{:S(2)}) copy-start(bf16[16,4096]{1,0:T(8,128)(2,1)} %emission_in.1) | copy-start | bytes 393220
  3.8 0.9 %copy-start.2 = (bf16[1,1,4,4,4096]{4,3,2,1,0:T(4,128)(2,1)S(1)}, bf16[1,1,4,4,4096]{4,3,2,1,0:T(4,128)(2,1)}, u32[]{:S(2)}) copy-start(bf16[1,1,4,4,4096]{4,3,2,1,0:T(4,128)(2,1)} %param.11) | copy-start | bytes 393220
  4.7 0.7 copy-start.3
  32.1 4.0 %copy-start = (bf16[64,128,128]{2,1,0:T(8,128)(2,1)S(1)}, bf16[64,128,128]{2,1,0:T(8,128)(2,1)}, u32[]{:S(2)}) copy-start(bf16[64,128,128]{2,1,0:T(8,128)(2,1)} %get-tuple-element.18.adj_form) | copy-start | bytes 6291460
